TPU v7x, 128 devices: a whole 4x4x4 slice. The times are simulated.
128 devices in a mesh: dp: 8 (over x, core), tensor: 16 (over z, y).
Axes of the slice: x: 4, y: 4, z: 4, core: 2. Of those that a mesh axis runs over, the one named last changes fastest.
Arguments:
- hidden_in: bfloat16 [16384, 4096], P(('dp', 'tensor')), parts along dimension 0, may hold values from -6 to 6
- norm_gain: bfloat16 [4096], replicated, may hold values from 0.099609375 to 1.8984375
- w_query: bfloat16 [4096, 4096], P(None, 'tensor'), may hold values from -0.09375 to 0.09375
- keyvalue_weight: bfloat16 [4096, 2048], P(None, 'tensor'), may hold values from -0.09375 to 0.09375
- w_out: bfloat16 [4096, 4096], P('tensor'), may hold values from -0.09375 to 0.09375
- prefix_keyvalue_cache: bfloat16 [4096, 2048], P(None, 'tensor'), may hold values from -600 to 600, as said below
- seg_ids: int32 [16384], P('dp'), parts along dimension 0, may hold values from 0 to 127, never falling along the last dimension, each value on 1 to 64 neighbouring positions
- seg_doc: int32 [1024], P('dp'), parts along dimension 0, may hold values from 0 to 15
- doc_lens: int32 [16], replicated, may hold values from 1 to 1024, 4096 in all
Outputs:
- mixed: bfloat16 [16384, 4096], P(('dp', 'tensor')), parts along dimension 0
There are 8 independent parts, one for each index of `dp`. A program takes and returns all parts, laid end to end along the dimension named above; an argument that names none is the same for every part. Nothing has to cross between parts.
Inputs may be any that keep to these rules, and one draw needn't show every extreme that they name: `seg_ids`: segment numbers never fall along the tokens; each of the 128 samples holds 1 to 64 tokens, one exactly 64. `doc_lens`: the documents fill the prefix end to end in order, lengths summing to 4096, the longest exactly 1024. `prefix_keyvalue_cache`: cached keys already carry the rotary map of their prefix positions.
All inputs are finite; a program needn't handle non-finite values.
Results may differ from a plain program's by a relative error of at most 0.028.
The roundings to bfloat16 on the way count: a program that leaves them out, or rounds other values in their place, can miss the bound.
Values may be sent and summed in bfloat16 or wider, within the bound.
A program may use at most 192 MiB of HBM per device.

v0:
```python
import math

import jax
import jax.numpy as jnp
from jax import lax
from jax.sharding import PartitionSpec as P

HEAD_SIZE = 128


eps = 1e-05
rope_theta = 500000.0


def from_partner(x, axis, bit):
    return lax.ppermute(x, axis, [(i, i ^ 1 << bit) for i in range(lax.axis_size(axis))])


def normalize(rows_in, gain):
    values = rows_in.astype(jnp.float32)
    mean_square = jnp.mean(values * values, axis=-1, keepdims=True)
    return (values * lax.rsqrt(mean_square + eps) * gain.astype(jnp.float32)).astype(jnp.bfloat16)


def rotary_tables(positions, head_dim):
    half_dim = head_dim // 2
    inverse = rope_theta ** (-(jnp.arange(half_dim, dtype=jnp.float32) * 2.0 / head_dim))
    angles = positions.astype(jnp.float32)[:, None] * inverse[None, :]
    return (jnp.cos(angles), jnp.sin(angles))


def apply_rotation(vectors, cosine_table, sine_table):
    half_dim = vectors.shape[-1] // 2
    lower_half = vectors[..., :half_dim]
    upper_half = vectors[..., half_dim:]
    cos_part = cosine_table[:, None, :]
    sin_part = sine_table[:, None, :]
    return jnp.concatenate(
        [
            lower_half * cos_part - upper_half * sin_part,
            upper_half * cos_part + lower_half * sin_part,
        ],
        axis=-1,
    )


def token_tables(seg_ids, seg_doc, doc_lens, prefix_len):
    token_count = seg_ids.shape[0]
    token_order = jnp.arange(token_count, dtype=jnp.int32)
    seg_start = jnp.sum(
        (seg_ids[None, :] < seg_ids[:, None]).astype(jnp.int32), axis=1, dtype=jnp.int32
    )
    positions = prefix_len + token_order - seg_start
    segments = jnp.arange(seg_doc.shape[0], dtype=jnp.int32)
    tok_doc = jnp.sum(
        jnp.where(seg_ids[:, None] == segments[None, :], seg_doc[None, :], 0),
        axis=1,
        dtype=jnp.int32,
    )
    doc_ends = jnp.cumsum(doc_lens, dtype=jnp.int32)
    prefix_order = jnp.arange(prefix_len, dtype=jnp.int32)
    key_doc = jnp.sum(
        (doc_ends[None, :] <= prefix_order[:, None]).astype(jnp.int32), axis=1, dtype=jnp.int32
    )
    return (positions, tok_doc, key_doc)


def attend_block(query_matrix, all_keys, all_values, allowed, score_scale):
    scores = (
        jnp.einsum("bmgd,kmd->bmgk", query_matrix, all_keys, preferred_element_type=jnp.float32)
        * score_scale
    )
    scores = jnp.where(allowed[:, None, None, :], scores, -1e30)
    row_max = jnp.max(scores, axis=-1, keepdims=True)
    weights = jnp.exp(scores - row_max)
    row_total = jnp.sum(weights, axis=-1, keepdims=True)
    weights_bf = (weights / row_total).astype(jnp.bfloat16)
    return jnp.einsum(
        "bmgk,kmd->bmgd", weights_bf, all_values, preferred_element_type=jnp.float32
    ).astype(jnp.bfloat16)


def local(
    hidden_in,
    norm_gain,
    w_query,
    keyvalue_weight,
    w_out,
    prefix_keyvalue_cache,
    seg_ids,
    seg_doc,
    doc_lens,
):
    tokens_all = seg_ids.shape[0]
    prefix_len = prefix_keyvalue_cache.shape[0]
    query_cols = w_query.shape[1]
    head_dim = HEAD_SIZE
    heads_here = query_cols // head_dim
    kv_here = 1
    group_width = heads_here // kv_here
    even_rank = lax.axis_index("tensor") % 2 == 0
    normalized_input = normalize(hidden_in, norm_gain)
    positions, tok_doc, key_doc = token_tables(seg_ids, seg_doc, doc_lens, prefix_len)
    cosine_table, sine_table = rotary_tables(positions, head_dim)
    weight_list = (w_query, keyvalue_weight)
    shard_rows = lax.all_gather(normalized_input, "tensor", axis=0, tiled=True)
    projected = jnp.concatenate(
        [jnp.dot(shard_rows, matrix, preferred_element_type=jnp.float32) for matrix in weight_list],
        axis=1,
    )
    query_projected = projected[:, :query_cols].reshape(tokens_all, heads_here, head_dim)
    query_matrix = apply_rotation(query_projected, cosine_table, sine_table).astype(jnp.bfloat16)
    kv_part = projected[:, query_cols:]
    own_part = kv_part.reshape(tokens_all, 1, head_dim)
    own_part = jnp.where(
        even_rank, apply_rotation(own_part, cosine_table, sine_table), own_part
    ).astype(jnp.bfloat16)
    partner_part, partner_cache = from_partner((own_part, prefix_keyvalue_cache), "tensor", 0)
    keys_new = jnp.where(even_rank, own_part, partner_part)
    values_new = jnp.where(even_rank, partner_part, own_part)
    cache_keys = jnp.where(even_rank, prefix_keyvalue_cache, partner_cache)
    cache_values = jnp.where(even_rank, partner_cache, prefix_keyvalue_cache)
    cache_keys = cache_keys.reshape(prefix_len, 1, head_dim)
    cache_values = cache_values.reshape(prefix_len, 1, head_dim)
    all_keys = jnp.concatenate([cache_keys, keys_new], axis=0)
    all_values = jnp.concatenate([cache_values, values_new], axis=0)
    block_rows = min(256, tokens_all)
    score_scale = 1.0 / math.sqrt(head_dim)
    token_order = jnp.arange(tokens_all, dtype=jnp.int32)

    def one_block(block_index):
        first_row = block_index * block_rows
        query_rows = lax.dynamic_slice_in_dim(query_matrix, first_row, block_rows, 0).reshape(
            block_rows, kv_here, group_width, head_dim
        )
        row_docs = lax.dynamic_slice_in_dim(tok_doc, first_row, block_rows, 0)
        row_segs = lax.dynamic_slice_in_dim(seg_ids, first_row, block_rows, 0)
        places = first_row + jnp.arange(block_rows, dtype=jnp.int32)
        prefix_ok = key_doc[None, :] == row_docs[:, None]
        own_ok = (seg_ids[None, :] == row_segs[:, None]) & (token_order[None, :] <= places[:, None])
        allowed = jnp.concatenate([prefix_ok, own_ok], axis=1)
        return attend_block(query_rows, all_keys, all_values, allowed, score_scale)

    attended = lax.map(one_block, jnp.arange(tokens_all // block_rows, dtype=jnp.int32)).reshape(
        tokens_all, query_cols
    )
    summed = lax.psum_scatter(
        jnp.dot(attended, w_out, preferred_element_type=jnp.float32).astype(jnp.bfloat16),
        "tensor",
        scatter_dimension=0,
        tiled=True,
    ).astype(jnp.float32)
    return (hidden_in.astype(jnp.float32) + summed).astype(jnp.bfloat16)


def solution(mesh):
    return jax.shard_map(
        local,
        mesh=mesh,
        in_specs=(
            P(("dp", "tensor"), None),
            P(),
            P(None, "tensor"),
            P(None, "tensor"),
            P("tensor", None),
            P(None, "tensor"),
            P("dp"),
            P("dp"),
            P(),
        ),
        out_specs=P(("dp", "tensor"), None),
        check_vma=False,
    )
```

profile of v0, /device:TPU:0, one launch (start us, length us, event | category | flops | bytes accessed | tf_op | source)
XLA Modules:
  0.0 425.1 jit_solution(10307681358659847505)
XLA Ops:
  9.0 2.5 fusion.27
  16.2 5.7 %multiply_cosine_fusion = (f32[2048,64]{1,0:T(8,128)}, f32[2048,64]{1,0:T(8,128)}) fusion(f32[64]{0:T(128)S(1)} %negate_power_fusion, f32[2048]{0:T(1024)S(1)} %subtract_convert_fusion.1), kind=kLoop, calls=%fused_computation.33 | loop fusion | flops 131072 | bytes 1057024 | tf_op jit(solution)/shard_map/cos | solution.py:29
  22.0 25.6 %collective-permute-done = bf16[4096,128]{1,0:T(8,128)(2,1)} collective-permute-done((bf16[4096,128]{1,0:T(8,128)(2,1)S(1)}, bf16[4096,128]{1,0:T(8,128)(2,1)}, u32[]{:S(2)}, u32[]{:S(2)}) %collective-permute-start) | collective-permute-done | bytes 1048608 | tf_op jit(solution)/shard_map/ppermute | solution.py:16
  47.5 2.7 select_bitcast_fusion
  50.2 85.4 %all-gather.2.cloned.1.call-done = bf16[2048,4096]{1,0:T(8,128)(2,1)} async-done(((bf16[128,4096]{1,0:T(8,128)(2,1)}), bf16[2048,4096]{1,0:T(8,128)(2,1)}) %all-gather.2.cloned.1.call-update) | async-done | bytes 16777232 | tf_op jit(solution)/shard_map/all_gather | solution.py:106
  135.7 12.2 %fusion.41 = f32[2048,256]{0,1:T(8,128)} fusion(bf16[2048,4096]{1,0:T(8,128)(2,1)} %all-gather.2.cloned.1.call-done, bf16[4096,256]{1,0:T(8,128)(2,1)} %param.13), kind=kOutput, calls=%fused_computation.61 | convolution fusion | flops 4294967296 | bytes 20971520 | tf_op jit(solution)/shard_map/dot_general | solution.py:108
  147.9 3.1 fusion.40
  151.0 11.7 %fusion.42 = f32[2048,128]{0,1:T(8,128)S(1)} fusion(bf16[2048,4096]{1,0:T(8,128)(2,1)} %all-gather.2.cloned.1.call-done, bf16[4096,128]{1,0:T(8,128)(2,1)} %param.14), kind=kOutput, calls=%fused_computation.62 | convolution fusion | flops 2147483648 | bytes 18874368 | tf_op jit(solution)/shard_map/dot_general | solution.py:108
  167.3 3.2 copy.28
  172.4 3.3 subtract_convert_fusion
  177.3 2.5 collective-permute-done.1
  186.2 3.4 pad_maximum_fusion
  189.6 103.3 %while.11 = (s32[]{:T(128)}, bf16[8,256,1,2,128]{4,1,3,2,0:T(8,128)(2,1)}, s32[4096]{0:T(1024)S(1)}, s32[8]{0:T(128)S(1)}, s32[2048]{0:T(1024)S(1)}, /*index=5*/...) while((s32[]{:T(128)}, ...), condition=%wide.region_8.9_spmd.clone, body=%wide.region_5.8_spmd.clone.sunk | while | flops 1640037632 | bytes 60074252 | solution.py:144
  193.1 3.8 fusion.58
  198.9 3.6 fusion.60
  206.0 3.8 fusion.58
  211.8 3.6 fusion.60
  218.9 3.8 fusion.58
  224.7 3.6 fusion.60
  231.9 3.8 fusion.58
  237.6 3.6 fusion.60
  244.8 3.8 fusion.58
  250.5 3.6 fusion.60
  257.7 3.8 fusion.58
  263.4 3.6 fusion.60
  270.6 3.8 fusion.58
  276.4 3.6 fusion.60
  283.5 3.8 fusion.58
  289.3 3.6 fusion.60
  292.9 2.7 copy.26
  297.1 8.2 %convolution_convert_fusion = bf16[2048,4096]{1,0:T(8,128)(2,1)} fusion(bf16[2048,256]{0,1:T(8,128)(2,1)S(1)} %bitcast.77, bf16[256,4096]{1,0:T(8,128)(2,1)S(1)} %copy-done), kind=kOutput, calls=%fused_computation.20 | convolution fusion | flops 4303355904 | bytes 19922944 | tf_op jit(solution)/shard_map/dot_general | solution.py:148
  305.3 110.5 %reduce-scatter.2.cloned.1.call-done = bf16[128,4096]{1,0:T(8,128)(2,1)} async-done(((bf16[2048,4096]{1,0:T(8,128)(2,1)}), bf16[128,4096]{1,0:T(8,128)(2,1)}) %reduce-scatter.2.cloned.1.call-update) | async-done | bytes 1048592 | tf_op jit(solution)/shard_map/reduce_scatter | solution.py:147
  (140 shorter events, 64.1 us)
Async XLA Ops:
  6.5 290.5 %copy-start = (bf16[256,4096]{1,0:T(8,128)(2,1)S(1)}, bf16[256,4096]{1,0:T(8,128)(2,1)}, u32[]{:S(2)}) copy-start(bf16[256,4096]{1,0:T(8,128)(2,1)} %param.15) | copy-start | bytes 6291460
  6.5 5.1 %copy-start.6 = (bf16[4096,128]{1,0:T(8,128)(2,1)S(1)}, bf16[4096,128]{1,0:T(8,128)(2,1)}, u32[]{:S(2)}) copy-start(bf16[4096,128]{1,0:T(8,128)(2,1)} %param.16) | copy-start | bytes 3145732
  6.5 6.8 %copy-start.8 = (s32[16]{0:T(128)S(1)}, s32[16]{0:T(128)}, u32[]{:S(2)}) copy-start(s32[16]{0:T(128)} %param.19) | copy-start | bytes 196
  6.5 7.2 %copy-start.7 = (s32[2048]{0:T(1024)S(1)}, s32[2048]{0:T(1024)}, u32[]{:S(2)}) copy-start(s32[2048]{0:T(1024)} %param.17) | copy-start | bytes 24580
  6.5 7.2 %copy-start.9 = (s32[128]{0:T(128)S(1)}, s32[128]{0:T(128)}, u32[]{:S(2)}) copy-start(s32[128]{0:T(128)} %param.18) | copy-start | bytes 1540
  6.5 129.1 %all-gather.2.cloned.1.call-start = ((), (), s32[]{:S(2)}) async-start(), calls=%async_computation.1 | async-start | bytes 17825792 | tf_op jit(solution)/shard_map/all_gather | solution.py:106
  11.5 404.3 %reduce-scatter.2.cloned.1.call-start = ((), (), s32[]{:S(2)}) async-start(), calls=%async_computation.2 | async-start | bytes 17825792 | tf_op jit(solution)/shard_map/reduce_scatter | solution.py:147
  11.6 35.9 %collective-permute-start = (bf16[4096,128]{1,0:T(8,128)(2,1)S(1)}, bf16[4096,128]{1,0:T(8,128)(2,1)}, u32[]{:S(2)}, u32[]{:S(2)}) collective-permute-start(bf16[4096,128]{1,0:T(8,128)(2,1)S(1)} %copy-done.6), channel_id=1, source_target_pairs={{0,1},{1,0},{2,3},{3,2},{4,5},{5,4},{6,7},{7,6},{8,9},{9,8},{10,11... | collective-permute-start | bytes 3145736 | tf_op jit(solution)/shard_map/ppermute | solution.py:16
  165.9 4.6 %copy-start.3 = (f32[2048,2,64]{0,2,1:T(8,128)S(1)}, f32[2048,2,64]{0,2,1:T(8,128)}, u32[]{:S(2)}) copy-start(f32[2048,2,64]{0,2,1:T(8,128)} %get-tuple-element.103) | copy-start | bytes 3145732
  165.9 13.9 %collective-permute-start.1 = (bf16[2048,1,128]{0,2,1:T(8,128)(2,1)}, bf16[2048,1,128]{0,2,1:T(8,128)(2,1)}, u32[]{:S(2)}, u32[]{:S(2)}) collective-permute-start(bf16[2048,1,128]{0,2,1:T(8,128)(2,1)} %fusion.38), channel_id=1, source_target_pairs={{0,1},{1,0},{2,3},{3,2},{4,5},{5,4},{6,7},{7,6},{8,9},{9,8},{10,11... | collective-permute-start | bytes 1572872 | tf_op jit(solution)/shard_map/ppermute | solution.py:16
  177.3 8.9 %copy-start.2 = (bf16[4096,1,128]{2,0,1:T(8,128)(2,1)S(1)}, bf16[4096,1,128]{2,0,1:T(8,128)(2,1)}, u32[]{:S(2)}) copy-start(bf16[4096,1,128]{2,0,1:T(8,128)(2,1)} %get-tuple-element.100) | copy-start | bytes 3145732
  191.7 1.4 copy-start.4
  197.0 1.9 copy-start.5
  204.6 1.4 copy-start.4
  209.9 1.9 copy-start.5
  217.5 1.4 copy-start.4
  222.8 1.9 copy-start.5
  230.5 1.4 copy-start.4
  235.7 1.9 copy-start.5
  243.4 1.4 copy-start.4
  248.6 1.9 copy-start.5
  256.3 1.4 copy-start.4
  261.5 1.9 copy-start.5
  269.2 1.4 copy-start.4
  274.4 1.9 copy-start.5
  282.1 1.4 copy-start.4
  287.3 1.9 copy-start.5
  305.3 110.6 %copy-start.1 = (bf16[128,4096]{1,0:T(8,128)(2,1)S(1)}, bf16[128,4096]{1,0:T(8,128)(2,1)}, u32[]{:S(2)}) copy-start(bf16[128,4096]{1,0:T(8,128)(2,1)} %param.11) | copy-start | bytes 3145732
Sparse Core Ops, SparseCore 0:
  11.7 123.9 all-gather.1
  305.4 110.3 reduce-scatter.1
where the time goes:
time: 427 us; the launch traced here: 425 us
  waiting for transfers between devices  224 us (52%)
  matrix products  91.4 us (21%)
  other arithmetic  59.7 us (14%)
  local copies, waits for them, and re-layouts  27.7 us (6%)
  between operations  13.5 us (3%)
  loops' own time  5.44 us (1%)
    reduce_scatter x1, waiting for transfers between devices, local(): lax.psum_scatter(jnp.dot(attended, w_out, preferred_element_type=jnp.floa...  111 us
    all_gather x1, waiting for transfers between devices, local(): shard_rows = lax.all_gather(normalized_input, 'tensor', axis=0, tiled=True)  85.4 us
    dot_general x8, matrix products, attend_block(): jnp.einsum('bmgd,kmd->bmgk', query_matrix, all_keys, preferred_element_ty...  30.5 us
    dot_general x8, matrix products, attend_block(): jnp.einsum('bmgk,kmd->bmgd', weights_bf, all_values, preferred_element_ty...  28.8 us
    ppermute x2, waiting for transfers between devices, from_partner(): lax.ppermute(x, axis, [(i, i ^ 1 << bit) for i in range(lax.axis_size(axi...  28.1 us
    dot_general x2, matrix products, local(): jnp.dot(shard_rows, matrix, preferred_element_type=jnp.float32)  23.9 us
    reduce_sum x8, other arithmetic, attend_block(): row_total = jnp.sum(weights, axis=-1, keepdims=True)  15.4 us
  transfers between devices with their start and end apart: 4, of which 4 were waited for; matrix products, arithmetic and copies ran while one was open for 5% of the time, Pallas kernels for 0%

commit v1 on v0

v1 whole, which is shorter than its diff:
```python
import functools
import math

import jax
import jax.numpy as jnp
from jax import lax
from jax.experimental import pallas as pl
from jax.experimental.pallas import tpu as pltpu
from jax.sharding import PartitionSpec as P

HEAD = 128
HALO = 64
SIDE = 4
EPS = 1e-05
THETA = 500000.0
MASKED = -1e30
MESH = pl.DeviceIdType.MESH
BF16 = jnp.bfloat16
F32 = jnp.float32


def place():
    dp, tensor = lax.axis_index("dp"), lax.axis_index("tensor")
    return dp // 2, dp % 2, tensor // SIDE, tensor % SIDE


def device(x, core, z, y):
    return (2 * (x % SIDE) + core, SIDE * (z % SIDE) + y % SIDE)


def greet(others):
    barrier = pltpu.get_barrier_semaphore()
    for other in others:
        pl.semaphore_signal(barrier, inc=1, device_id=other, device_id_type=MESH)
    pl.semaphore_wait(barrier, len(others))


def remote(src, dst, send, recv, other):
    return pltpu.make_async_remote_copy(
        src_ref=src, dst_ref=dst, send_sem=send, recv_sem=recv, device_id=other, device_id_type=MESH
    )


def rotate(v, cos, sin):
    return v * cos + pltpu.roll(v, HEAD // 2, 1) * sin


class Spread:
    def __init__(self, own, block, send, recv):
        self.own, self.block, self.send, self.recv = own, block, send, recv
        self.x, self.core, self.z, self.y = place()

    def number(self, parity, core, half):
        return 4 * parity + 2 * core + half

    def up(self, n):
        return (self.x, self.core, self.z, self.y + n)

    def copy(self, i, d, piece, to, first=False):
        slot = (self.y + d + SIDE) % SIDE
        src = self.own(piece) if first else self.block(slot, piece)
        return remote(
            src, self.block(slot, piece), self.send.at[i], self.recv.at[i], device(*to)
        )

    def mine(self, half):
        return self.number(self.x % 2, self.core, half)

    def sends(self, i):
        if i in (0, 1):
            return self.copy(i, 0, self.mine(i), self.up(1), True)
        if i == 2:
            return self.copy(i, 3, self.mine(0), self.up(1))
        if i in (3, 4):
            return self.copy(i, 0, self.mine(4 - i), self.up(SIDE - 1), True)
        if i == 5:
            return self.copy(i, 1, self.mine(1), self.up(SIDE - 1))
        d, half = 1 + (i % 6) // 2, i % 2
        if i < 12:
            to = (self.x + (SIDE - 1 if half else 1), self.core, self.z, self.y)
            return self.copy(i, d, self.mine(half), to)
        parity = self.x % 2 if i < 18 else 1 - self.x % 2
        piece = self.number(parity, self.core, half)
        return self.copy(i, d, piece, (self.x, 1 - self.core, self.z, self.y))

    def got(self, i):
        if i < 6:
            d = {0: 3, 1: 3, 2: 2, 3: 1, 4: 1, 5: 2}[i]
            half = {0: 0, 1: 1, 2: 0, 3: 1, 4: 0, 5: 1}[i]
            piece = self.mine(half)
        else:
            d, half = 1 + (i % 6) // 2, i % 2
            parity = self.x % 2 if 12 <= i < 18 else 1 - self.x % 2
            core = self.core if i < 12 else 1 - self.core
            piece = self.number(parity, core, half)
        view = self.block((self.y + d) % SIDE, piece)
        remote(view, view, self.send.at[i], self.recv.at[i], device(*self.up(1))).wait_recv()

    def start(self):
        for i in (0, 3, 1, 4):
            self.sends(i).start()

    def along_y(self, i):
        self.got(i)
        if i == 0:
            self.sends(2).start()
        if i == 3:
            self.sends(5).start()
        d = {0: 3, 1: 3, 2: 2, 3: 1, 4: 1, 5: 2}[i]
        half = {0: 0, 1: 1, 2: 0, 3: 1, 4: 0, 5: 1}[i]
        self.sends(6 + 2 * (d - 1) + half).start()
        self.sends(12 + 2 * (d - 1) + half).start()

    def along_x(self, i):
        self.got(i)
        self.sends(i + 12).start()

    def sibling(self):
        for i in range(12, 24):
            self.got(i)

    def sent(self):
        for i in range(24):
            self.sends(i).wait_send()


Y_ORDER = (0, 3, 1, 4, 2, 5)
X_ORDER = (10, 7, 11, 6, 8, 9)


def gather_project(
    hid, gain, cos, sin, wq, wkv, pfx, wo,
    q_out, kv, pfx_all, wo_all,
    xs, wqs, wkvs, send, recv, x_send, x_recv, halo_send, halo_recv, local,
):
    x, core, z, y = place()
    here = lambda dx, dcore, dz, dy: device(
        x + dx, core if dcore == 0 else 1 - core, z + dz, y + dy
    )
    down = SIDE - 1
    greet([
        here(0, 0, 0, 1), here(0, 0, 0, down), here(0, 0, 1, 0), here(0, 0, down, 0),
        here(1, 0, 0, 0), here(down, 0, 0, 0), here(0, 1, 0, 0),
    ])

    def rows(array, count):
        return lambda n: array.at[pl.ds(pl.multiple_of(n * count, count), count), :]

    def blocks(array, count):
        return lambda s, n: array.at[s, pl.ds(pl.multiple_of(n * count, count), count), :]

    spreads = [
        Spread(rows(own, count), blocks(every, count), send.at[k], recv.at[k])
        for k, (own, every, count) in enumerate(
            [(wkv, wkvs, 512), (wq, wqs, 512), (pfx, pfx_all, 512), (wo, wo_all, 32)]
        )
    ]
    skv, sq, sp, so = spreads
    skv.start()
    sq.start()

    values = hid[...].astype(F32)
    scale = lax.rsqrt(jnp.mean(values * values, axis=-1, keepdims=True) + EPS)
    xs[z] = (values * scale * gain[...].astype(F32)).astype(BF16)

    def x_send_copy(i):
        slot = {0: z, 1: z, 2: z + 3, 3: z, 4: z, 5: z + 1}[i] % SIDE
        half = {0: 0, 1: 1, 2: 0, 3: 1, 4: 0, 5: 1}[i]
        to = here(0, 0, 1, 0) if i < 3 else here(0, 0, down, 0)
        view = xs.at[slot, pl.ds(64 * half, 64), :]
        return remote(view, view, x_send.at[i], x_recv.at[i], to)

    def x_got(i):
        slot = {0: z + 3, 1: z + 3, 2: z + 2, 3: z + 1, 4: z + 1, 5: z + 2}[i] % SIDE
        half = {0: 0, 1: 1, 2: 0, 3: 1, 4: 0, 5: 1}[i]
        view = xs.at[slot, pl.ds(64 * half, 64), :]
        remote(view, view, x_send.at[i], x_recv.at[i], here(0, 0, 1, 0)).wait_recv()

    for i in (0, 3, 1, 4):
        x_send_copy(i).start()
    stays = [
        pltpu.make_async_copy(own, every.at[y], local.at[k])
        for k, (own, every) in enumerate([(wkv, wkvs), (wq, wqs), (pfx, pfx_all), (wo, wo_all)])
    ]
    for copy in stays:
        copy.start()

    for i in (0, 3):
        skv.along_y(i)
    for i in (0, 3):
        x_got(i)
        x_send_copy(i + 2).start()
    for i in (1, 4, 2, 5):
        skv.along_y(i)
    for i in (0, 3):
        sq.along_y(i)
    for i in X_ORDER:
        skv.along_x(i)
    sp.start()
    for i in (1, 4, 2, 5):
        sq.along_y(i)
    for i in (0, 3):
        sp.along_y(i)
    for i in X_ORDER:
        sq.along_x(i)
    so.start()
    for i in (1, 4, 2, 5):
        x_got(i)
    skv.sibling()
    sq.sibling()
    stays[0].wait()
    stays[1].wait()

    half_rows = 2 * 128

    def project_kv():
        for s in range(SIDE):
            @pl.loop(0, 2)
            def _(m):
                tall = pl.ds(pl.multiple_of(m * half_rows, half_rows), half_rows)
                lhs = xs[pl.ds(2 * m, 2)].reshape(half_rows, xs.shape[2])
                got = jnp.dot(lhs, wkvs[s], preferred_element_type=F32)
                if s % 2 == 0:
                    got = rotate(got, cos[tall, :], sin[tall, :])
                got = got.astype(BF16).reshape(2, 128, HEAD)
                kv[pl.ds(2 * m, 2), pl.ds(HALO, 128), pl.ds(HEAD * s, HEAD)] = got

    def project_q(s):
        @pl.loop(0, 2)
        def _(m):
            tall = pl.ds(pl.multiple_of(m * half_rows, half_rows), half_rows)
            lhs = xs[pl.ds(2 * m, 2)].reshape(half_rows, xs.shape[2])
            got = jnp.dot(lhs, wqs[s], preferred_element_type=F32)
            for n in range(2):
                one = rotate(got[:, HEAD * n : HEAD * (n + 1)], cos[tall, :], sin[tall, :])
                q_out[tall, pl.ds(HEAD * (2 * s + n), HEAD)] = one.astype(BF16)

    def halo_copy(slot):
        dst = (slot + y // 3) % SIDE
        return remote(
            kv.at[slot, pl.ds(128, HALO), :],
            kv.at[dst, pl.ds(0, HALO), :],
            halo_send.at[slot],
            halo_recv.at[slot],
            here(0, 0, 0, 1),
        )

    project_kv()
    for slot in range(SIDE):
        halo_copy(slot).start()
    for i in (1, 4, 2, 5):
        sp.along_y(i)
    project_q(0)
    for i in (0, 3):
        so.along_y(i)
    for i in X_ORDER[:4]:
        sp.along_x(i)
    project_q(1)
    for i in X_ORDER[4:]:
        sp.along_x(i)
    for i in (1, 4):
        so.along_y(i)
    project_q(2)
    for i in (2, 5):
        so.along_y(i)
    project_q(3)
    for i in X_ORDER:
        so.along_x(i)
    sp.sibling()
    so.sibling()
    stays[2].wait()
    stays[3].wait()
    for slot in range(SIDE):
        halo_copy(slot).wait()
    for i in range(6):
        x_send_copy(i).wait_send()
    for spread in spreads:
        spread.sent()


def attend(
    bounds, rank_row, rank_col, meta, key_doc, key_seg, key_pos, q, kv, pfx,
    out, perm, qs, ms, outs, top, total, acc,
):
    tokens = q.shape[0]
    order = lax.broadcasted_iota(jnp.int32, (tokens, tokens), 0)
    perm[...] = (rank_row[...] == order).astype(F32).astype(BF16)
    qs[...] = jnp.dot(perm[...], q[...], preferred_element_type=F32).astype(BF16)
    ms[...] = jnp.dot(perm[...], meta[...], preferred_element_type=F32)
    tile, keys, group = 128, 256, 4
    score_scale = 1.0 / math.sqrt(HEAD)

    @pl.loop(0, tokens // tile)
    def _(i):
        rows = pl.ds(pl.multiple_of(i * tile, tile), tile)
        top[...] = jnp.full(top.shape, MASKED, F32)
        total[...] = jnp.zeros(total.shape, F32)
        acc[...] = jnp.zeros(acc.shape, F32)
        queries = [
            jnp.concatenate(
                [qs[rows, pl.ds(HEAD * (group * h + n), HEAD)] for n in range(group)], axis=0
            )
            for h in range(2)
        ]

        def step(key, value, allowed):
            bias = jnp.where(allowed, 0.0, MASKED)
            for h in range(2):
                s = lax.dot_general(
                    queries[h], key[h], (((1,), (1,)), ((), ())), preferred_element_type=F32
                )
                s = s * score_scale
                s = jnp.where(
                    jnp.broadcast_to((bias < 0.0)[None], (group, tile, keys)),
                    MASKED,
                    s.reshape(group, tile, keys),
                ).reshape(group * tile, keys)
                old = top[h, :, :1]
                new = jnp.maximum(old, jnp.max(s, axis=-1, keepdims=True))
                p = jnp.exp(s - new)
                fade = jnp.exp(old - new)
                top[h] = jnp.broadcast_to(new, top.shape[1:])
                total[h] = total[h] * fade + jnp.sum(p, axis=-1, keepdims=True)
                acc[h] = acc[h] * fade + jnp.dot(
                    p.astype(BF16), value[h], preferred_element_type=F32
                )

        seg, pos, doc = ms[rows, 1:2], ms[rows, 2:3], ms[rows, 0:1]

        @pl.loop(0, kv.shape[0] // keys)
        def _(j):
            cut = pl.ds(pl.multiple_of(j * keys, keys), keys)
            allowed = (key_seg[j] == seg) & (key_pos[j] <= pos)
            step(
                [kv[cut, pl.ds(2 * HEAD * h, HEAD)] for h in range(2)],
                [kv[cut, pl.ds(2 * HEAD * h + HEAD, HEAD)] for h in range(2)],
                allowed,
            )

        @pl.loop(bounds[i], bounds[SIDE + i])
        def _(j):
            cut = pl.ds(pl.multiple_of(j * keys, keys), keys)
            allowed = key_doc[j] == doc
            step(
                [pfx[2 * h, cut, :] for h in range(2)],
                [pfx[2 * h + 1, cut, :] for h in range(2)],
                allowed,
            )

        for h in range(2):
            done = (acc[h] / total[h]).astype(BF16)
            for n in range(group):
                outs[rows, pl.ds(HEAD * (group * h + n), HEAD)] = done[n * tile : (n + 1) * tile]

    order = lax.broadcasted_iota(jnp.int32, (tokens, tokens), 1)
    perm[...] = (rank_col[...] == order).astype(F32).astype(BF16)
    out[...] = jnp.dot(perm[...], outs[...], preferred_element_type=F32).astype(BF16)


COLS = 512


def project_reduce(
    att, wo, hid, mixed,
    far_out, near_out, far_in, near_in, far_send, far_recv, near_send, near_recv,
):
    x, core, z, y = place()
    sides = [device(x, core, z + 1, y), device(x, core, z + SIDE - 1, y)]
    greet(sides)
    chunks = wo.shape[1] // COLS

    def partial(slot, j):
        return jnp.dot(
            att[slot % SIDE], wo[:, pl.ds(COLS * j, COLS)], preferred_element_type=F32
        )

    def far(j):
        return remote(
            far_out.at[j], far_in.at[j], far_send.at[j], far_recv.at[j], sides[j % 2]
        )

    def near(side, j):
        return remote(
            near_out.at[side, j],
            near_in.at[side, j],
            near_send.at[side, j],
            near_recv.at[side, j],
            sides[side],
        )

    for j in range(chunks):
        far_out[j] = partial(z + 2, j).astype(BF16)
        far(j).start()
    for j in range(chunks):
        side = 1 - j % 2
        near_out[side, j] = partial(z + (3 if side else 1), j).astype(BF16)
        near(side, j).start()
        side = j % 2
        mine = partial(z + (3 if side else 1), j)
        far(j).wait_recv()
        near_out[side, j] = (mine + far_in[j].astype(F32)).astype(BF16)
        near(side, j).start()
    for j in range(chunks):
        cut = pl.ds(COLS * j, COLS)
        mine = partial(z, j) + hid[:, cut].astype(F32)
        near(0, j).wait_recv()
        near(1, j).wait_recv()
        mine = mine + near_in[0, j].astype(F32) + near_in[1, j].astype(F32)
        mixed[:, cut] = mine.astype(BF16)
    for j in range(chunks):
        far(j).wait_send()
        near(0, j).wait_send()
        near(1, j).wait_send()


def tables(seg_ids, seg_doc, doc_lens, prefix_len):
    y = lax.axis_index("tensor") % SIDE
    padded = jnp.concatenate([jnp.full((HALO,), -1, jnp.int32), seg_ids])
    span = HALO + 128
    starts = [128 * (SIDE * s + y) for s in range(SIDE)]
    key_seg = jnp.concatenate([lax.dynamic_slice_in_dim(padded, a, span) for a in starts])
    places = jnp.concatenate([a - HALO + jnp.arange(span, dtype=jnp.int32) for a in starts])
    before = jnp.sum((seg_ids[None, :] < key_seg[:, None]).astype(jnp.int32), axis=1)
    key_pos = places - before
    seg = key_seg.reshape(SIDE, span)[:, HALO:].reshape(-1)
    pos = key_pos.reshape(SIDE, span)[:, HALO:].reshape(-1)
    segments = jnp.arange(seg_doc.shape[0], dtype=jnp.int32)
    doc = jnp.sum(jnp.where(seg[:, None] == segments[None, :], seg_doc[None, :], 0), axis=1)
    docs = jnp.arange(doc_lens.shape[0], dtype=jnp.int32)
    ends = jnp.sum(jnp.where(docs[None, :] <= docs[:, None], doc_lens[None, :], 0), axis=1)
    at = jnp.arange(prefix_len, dtype=jnp.int32)
    key_doc = jnp.sum((ends[None, :] <= at[:, None]).astype(jnp.int32), axis=1)
    order = doc * seg.shape[0] + jnp.arange(seg.shape[0], dtype=jnp.int32)
    rank = jnp.sum((order[None, :] < order[:, None]).astype(jnp.int32), axis=1)
    upto = jnp.sum((doc[None, :] <= docs[:, None]).astype(jnp.int32), axis=1)
    tile = jnp.arange(SIDE, dtype=jnp.int32) * 128
    first = jnp.sum((upto[None, :] <= tile[:, None]).astype(jnp.int32), axis=1)
    last = jnp.sum((upto[None, :] <= tile[:, None] + 127).astype(jnp.int32), axis=1)
    low = jnp.sum(jnp.where(docs[None, :] < first[:, None], doc_lens[None, :], 0), axis=1)
    high = jnp.sum(jnp.where(docs[None, :] <= last[:, None], doc_lens[None, :], 0), axis=1)
    bounds = jnp.concatenate([low // 256, (high + 255) // 256])
    return key_seg, key_pos, seg, pos, doc, key_doc, rank, bounds


def local(hidden_in, norm_gain, w_query, keyvalue_weight, w_out, cache, seg_ids, seg_doc, doc_lens):
    prefix_len = cache.shape[0]
    width = hidden_in.shape[1]
    key_seg, key_pos, seg, pos, doc, key_doc, rank, bounds = tables(
        seg_ids, seg_doc, doc_lens, prefix_len
    )
    half = HEAD // 2
    inverse = THETA ** (-(jnp.arange(half, dtype=F32) * 2.0 / HEAD))
    angles = (prefix_len + pos).astype(F32)[:, None] * inverse[None, :]
    cos, sin = jnp.cos(angles), jnp.sin(angles)
    cos = jnp.concatenate([cos, cos], axis=1)
    sin = jnp.concatenate([-sin, sin], axis=1)

    vmem = pl.BlockSpec(memory_space=pltpu.VMEM)
    smem = pl.BlockSpec(memory_space=pltpu.SMEM)
    whole = pl.BlockSpec(memory_space=pl.ANY)
    tokens = SIDE * 128
    q, kv, pfx, wo = pl.pallas_call(
        gather_project,
        out_shape=(
            jax.ShapeDtypeStruct((tokens, 8 * HEAD), BF16),
            jax.ShapeDtypeStruct((SIDE, HALO + 128, 4 * HEAD), BF16),
            jax.ShapeDtypeStruct((SIDE, prefix_len, HEAD), BF16),
            jax.ShapeDtypeStruct((SIDE,) + w_out.shape, BF16),
        ),
        in_specs=[vmem] * 4 + [whole] * 4,
        out_specs=(vmem, vmem, whole, whole),
        scratch_shapes=[
            pltpu.VMEM((SIDE, 128, width), BF16),
            pltpu.VMEM((SIDE,) + w_query.shape, BF16),
            pltpu.VMEM((SIDE,) + keyvalue_weight.shape, BF16),
            pltpu.SemaphoreType.DMA((4, 24)),
            pltpu.SemaphoreType.DMA((4, 24)),
            pltpu.SemaphoreType.DMA((6,)),
            pltpu.SemaphoreType.DMA((6,)),
            pltpu.SemaphoreType.DMA((4,)),
            pltpu.SemaphoreType.DMA((4,)),
            pltpu.SemaphoreType.DMA((4,)),
        ],
        compiler_params=pltpu.CompilerParams(
            collective_id=0, has_side_effects=True, vmem_limit_bytes=48 * 2**20
        ),
        name="gather_project",
    )(hidden_in, norm_gain[None, :], cos, sin, w_query, keyvalue_weight, cache, w_out)

    meta = jnp.stack([doc, seg, pos], axis=1).astype(BF16)
    meta = jnp.pad(meta, ((0, 0), (0, HEAD - 3)))
    attended = pl.pallas_call(
        attend,
        out_shape=jax.ShapeDtypeStruct((tokens, 8 * HEAD), BF16),
        in_specs=[smem] + [vmem] * 9,
        out_specs=vmem,
        scratch_shapes=[
            pltpu.VMEM((tokens, tokens), BF16),
            pltpu.VMEM((tokens, 8 * HEAD), BF16),
            pltpu.VMEM((tokens, HEAD), F32),
            pltpu.VMEM((tokens, 8 * HEAD), BF16),
            pltpu.VMEM((2, tokens, HEAD), F32),
            pltpu.VMEM((2, tokens, HEAD), F32),
            pltpu.VMEM((2, tokens, HEAD), F32),
        ],
        compiler_params=pltpu.CompilerParams(vmem_limit_bytes=32 * 2**20),
        name="attend",
    )(
        bounds,
        rank[None, :],
        rank[:, None],
        meta,
        key_doc.astype(F32).reshape(-1, 1, 256),
        key_seg.astype(F32).reshape(-1, 1, 256),
        key_pos.astype(F32).reshape(-1, 1, 256),
        q,
        kv.reshape(SIDE * (HALO + 128), 4 * HEAD),
        pfx,
    )

    chunks = width // COLS
    return pl.pallas_call(
        project_reduce,
        out_shape=jax.ShapeDtypeStruct(hidden_in.shape, BF16),
        in_specs=[vmem] * 3,
        out_specs=vmem,
        scratch_shapes=[
            pltpu.VMEM((chunks, 128, COLS), BF16),
            pltpu.VMEM((2, chunks, 128, COLS), BF16),
            pltpu.VMEM((chunks, 128, COLS), BF16),
            pltpu.VMEM((2, chunks, 128, COLS), BF16),
            pltpu.SemaphoreType.DMA((chunks,)),
            pltpu.SemaphoreType.DMA((chunks,)),
            pltpu.SemaphoreType.DMA((2, chunks)),
            pltpu.SemaphoreType.DMA((2, chunks)),
        ],
        compiler_params=pltpu.CompilerParams(
            collective_id=1, has_side_effects=True, vmem_limit_bytes=32 * 2**20
        ),
        name="project_reduce",
    )(attended.reshape(SIDE, 128, 8 * HEAD), wo.reshape(-1, width), hidden_in)


def solution(mesh):
    return jax.shard_map(
        local,
        mesh=mesh,
        in_specs=(
            P(("dp", "tensor"), None),
            P(),
            P(None, "tensor"),
            P(None, "tensor"),
            P("tensor", None),
            P(None, "tensor"),
            P("dp"),
            P("dp"),
            P(),
        ),
        out_specs=P(("dp", "tensor"), None),
        check_vma=False,
    )
```

time: 427 us -> 224 us (0.52)
  waiting for transfers between devices: 224 us -> 0 us
  Pallas kernels: 0 us -> 203 us
  matrix products: 91.4 us -> 0 us
  other arithmetic: 59.7 us -> 6.41 us
  local copies, waits for them, and re-layouts: 27.7 us -> 12.4 us
  between operations: 13.5 us -> 0.16 us
  loops' own time: 5.44 us -> 0 us
    pallas_call x0 -> x3, Pallas kernels: none -> 203 us  [the longest x1 85.6 us: local(): pl.pallas_call(gather_project, out_shape=(jax.ShapeDtypeStruct((tokens, 8...]
    reduce_scatter x1 -> x0, waiting for transfers between devices: 111 us -> none  [local(): lax.psum_scatter(jnp.dot(attended, w_out, preferred_element_type=jnp.floa...]
    dot_general x19 -> x0, matrix products: 91.4 us -> none  [the longest x8 30.5 us: attend_block(): jnp.einsum('bmgd,kmd->bmgk', query_matrix, all_keys, preferred_element_ty...]
    all_gather x1 -> x0, waiting for transfers between devices: 85.4 us -> none  [local(): shard_rows = lax.all_gather(normalized_input, 'tensor', axis=0, tiled=True)]
    ppermute x2 -> x0, waiting for transfers between devices: 28.1 us -> none  [from_partner(): lax.ppermute(x, axis, [(i, i ^ 1 << bit) for i in range(lax.axis_size(axi...]
    reduce_sum x12 -> x8, other arithmetic: 19.6 us -> 4.69 us  [the longest x1 1.45 us: tables(): jnp.sum((seg_ids[None, :] < key_seg[:, None]).astype(jnp.int32), axis=1)]
    concatenate x11 -> x3, other arithmetic: 8.24 us -> 0.35 us  [the longest x1 0.14 us: local(): sin = jnp.concatenate([-sin, sin], axis=1)]
    while x33 -> x0, local copies, waits for them, and re-layouts: 7.6 us -> none
  transfers between devices with their start and end apart: 4 -> 0, of which waited for: 4 -> 0; matrix products, arithmetic and copies ran while one was open for 5% -> 0% of each run, Pallas kernels for 0% -> 0%
where the time goes in v1:
time: 224 us; the launch traced here: 222 us
  Pallas kernels  203 us (91%)
  local copies, waits for them, and re-layouts  12.4 us (6%)
  other arithmetic  6.41 us (3%)
    pallas_call x1, Pallas kernels, local(): pl.pallas_call(gather_project, out_shape=(jax.ShapeDtypeStruct((tokens, 8...  85.6 us
    pallas_call x1, Pallas kernels, local(): pl.pallas_call(attend, out_shape=jax.ShapeDtypeStruct((tokens, 8 * HEAD),...  84.2 us
    pallas_call x1, Pallas kernels, local(): pl.pallas_call(project_reduce, out_shape=jax.ShapeDtypeStruct(hidden_in.s...  33.6 us
    unnamed x13, local copies, waits for them, and re-layouts  10.2 us

profile of v1, /device:TPU:0, one launch (start us, length us, event | category | flops | bytes accessed | tf_op | source)
XLA Modules:
  0.0 222.4 jit_solution(14389584489311563428)
XLA Ops:
  0.0 0.8 select_reduce_fusion.1
  0.8 0.9 pad_dynamic-slice_fusion.3
  1.8 0.1 fusion.3
  1.8 1.4 convert_reduce_fusion
  3.3 0.1 reshape.112
  3.4 0.1 fusion.1
  3.5 0.1 fusion.4
  3.5 0.9 select_reduce_fusion
  4.4 0.1 convert_reduce_fusion.3
  4.6 0.2 convert_reduce_fusion.5
  4.8 0.9 select_reduce_fusion.3
  5.7 0.1 pad_add_fusion.1.bounds
  5.8 0.2 convert_reduce_fusion.1
  6.0 0.1 sub.41
  6.1 0.1 convert_bitcast_fusion
  6.2 0.1 convert_reduce_fusion.2
  6.3 0.7 broadcast_in_dim.83.gain
  7.1 0.2 copy.16
  7.3 0.1 copy.17.rank_col
  7.4 1.0 fusion
  8.4 0.1 pad_maximum_fusion.1.sin
  8.6 0.1 pad_maximum_fusion.cos
  8.7 0.0 copy-start.2
  8.7 1.2 copy-done.2
  9.9 1.2 copy-done.3
  11.2 1.2 copy-done.4
  12.4 85.6 %gather_project.1 = (bf16[512,1024]{1,0:T(8,128)(2,1)S(1)}, bf16[4,192,512]{2,1,0:T(8,128)(2,1)S(1)}, bf16[4,4096,128]{2,1,0:T(8,128)(2,1)}, bf16[4,256,4096]{2,1,0:T(8,128)(2,1)}) custom-call(bf16[128,4096]{1,0:T(8,128)(2,1)S(1)} %copy-done.2, bf16[1,4096]{1,0:T(2,128)(2,1)S(1)} %broadcast_in_dim.83.gain, f32[512,128]{1,0:T(8,128)S(1)} %pad_maximum_fusion.cos, ...), custom_call_target="tpu_custom_call" | custom-call | tf_op jit(solution)/shard_map/gather_project/pallas_call | solution.py:462
  98.0 2.2 copy-done.1
  100.2 84.2 %attend.1 = bf16[512,1024]{1,0:T(8,128)(2,1)S(1)} custom-call(s32[8]{0:T(128)S(1)} %pad_add_fusion.1.bounds, s32[1,512]{1,0:T(1,128)S(1)} %bitcast.29, s32[512,1]{1,0:T(8,128)S(1)} %copy.17.rank_col, bf16[512,128]{1,0:T(8,128)(2,1)S(1)} %pad.5.meta, f32[16,1,256]{2,1,0:T(1,128)S(1)} %bitcast.27, f32[3,1,256]{2,1,0:T(1,128)S(1)} %convert_element_type.79.key_seg, ...), custom_call_target="tpu_custom_call" | custom-call | tf_op jit(solution)/shard_map/attend/pallas_call | solution.py:492
  184.4 3.4 %copy-done = bf16[4,256,4096]{2,1,0:T(8,128)(2,1)S(1)} copy-done((bf16[4,256,4096]{2,1,0:T(8,128)(2,1)S(1)}, bf16[4,256,4096]{2,1,0:T(8,128)(2,1)}, u32[]{:S(2)}) %copy-start) | copy-done | bytes 8388632
  187.8 33.6 %project_reduce.1 = bf16[128,4096]{1,0:T(8,128)(2,1)S(1)} custom-call(bf16[4,128,1024]{2,1,0:T(8,128)(2,1)S(1)} %bitcast.25, bf16[1024,4096]{1,0:T(8,128)(2,1)S(1)} %bitcast.24, bf16[128,4096]{1,0:T(8,128)(2,1)S(1)} %copy-done.2), custom_call_target="tpu_custom_call" | custom-call | tf_op jit(solution)/shard_map/project_reduce/pallas_call | solution.py:522
  221.4 1.0 copy.25
  (19 shorter events, 0.2 us)
Async XLA Ops:
  8.7 1.2 copy-start.2
  9.9 1.2 copy-start.3
  11.2 1.2 copy-start.4
  98.0 2.2 copy-start.1
  184.4 3.4 %copy-start = (bf16[4,256,4096]{2,1,0:T(8,128)(2,1)S(1)}, bf16[4,256,4096]{2,1,0:T(8,128)(2,1)}, u32[]{:S(2)}) copy-start(bf16[4,256,4096]{2,1,0:T(8,128)(2,1)} %get-tuple-element.12) | copy-start | bytes 25165828

commit v2 on v1

v2 whole, which is shorter than its diff:
```python
import functools
import math

import jax
import jax.numpy as jnp
import numpy as np
from jax import lax
from jax.experimental import pallas as pl
from jax.experimental.pallas import tpu as pltpu
from jax.sharding import PartitionSpec as P

HEAD = 128
HALO = 64
SIDE = 4
EPS = 1e-05
THETA = 500000.0
MASKED = -1e30
MESH = pl.DeviceIdType.MESH
BF16 = jnp.bfloat16
F32 = jnp.float32


def place():
    dp, tensor = lax.axis_index("dp"), lax.axis_index("tensor")
    return dp // 2, dp % 2, tensor // SIDE, tensor % SIDE


def device(x, core, z, y):
    return (2 * (x % SIDE) + core, SIDE * (z % SIDE) + y % SIDE)


def greet(others):
    barrier = pltpu.get_barrier_semaphore()
    for other in others:
        pl.semaphore_signal(barrier, inc=1, device_id=other, device_id_type=MESH)
    pl.semaphore_wait(barrier, len(others))


def remote(src, dst, send, recv, other):
    return pltpu.make_async_remote_copy(
        src_ref=src, dst_ref=dst, send_sem=send, recv_sem=recv, device_id=other, device_id_type=MESH
    )


def rotate(v, cos, sin):
    return v * cos + pltpu.roll(v, HEAD // 2, 1) * sin


class Spread:
    def __init__(self, own, block, send, recv):
        self.own, self.block, self.send, self.recv = own, block, send, recv
        self.x, self.core, self.z, self.y = place()

    def number(self, parity, core, half):
        return 4 * parity + 2 * core + half

    def up(self, n):
        return (self.x, self.core, self.z, self.y + n)

    def copy(self, i, d, piece, to, first=False):
        slot = (self.y + d + SIDE) % SIDE
        src = self.own(piece) if first else self.block(slot, piece)
        return remote(
            src, self.block(slot, piece), self.send.at[i], self.recv.at[i], device(*to)
        )

    def mine(self, half):
        return self.number(self.x % 2, self.core, half)

    def sends(self, i):
        if i in (0, 1):
            return self.copy(i, 0, self.mine(i), self.up(1), True)
        if i == 2:
            return self.copy(i, 3, self.mine(0), self.up(1))
        if i in (3, 4):
            return self.copy(i, 0, self.mine(4 - i), self.up(SIDE - 1), True)
        if i == 5:
            return self.copy(i, 1, self.mine(1), self.up(SIDE - 1))
        d, half = 1 + (i % 6) // 2, i % 2
        if i < 12:
            to = (self.x + (SIDE - 1 if half else 1), self.core, self.z, self.y)
            return self.copy(i, d, self.mine(half), to)
        parity = self.x % 2 if i < 18 else 1 - self.x % 2
        piece = self.number(parity, self.core, half)
        return self.copy(i, d, piece, (self.x, 1 - self.core, self.z, self.y))

    def got(self, i):
        if i < 6:
            d = {0: 3, 1: 3, 2: 2, 3: 1, 4: 1, 5: 2}[i]
            half = {0: 0, 1: 1, 2: 0, 3: 1, 4: 0, 5: 1}[i]
            piece = self.mine(half)
        else:
            d, half = 1 + (i % 6) // 2, i % 2
            parity = self.x % 2 if 12 <= i < 18 else 1 - self.x % 2
            core = self.core if i < 12 else 1 - self.core
            piece = self.number(parity, core, half)
        view = self.block((self.y + d) % SIDE, piece)
        remote(view, view, self.send.at[i], self.recv.at[i], device(*self.up(1))).wait_recv()

    def start(self):
        for i in (0, 3, 1, 4):
            self.sends(i).start()

    def along_y(self, i):
        self.got(i)
        if i == 0:
            self.sends(2).start()
        if i == 3:
            self.sends(5).start()
        d = {0: 3, 1: 3, 2: 2, 3: 1, 4: 1, 5: 2}[i]
        half = {0: 0, 1: 1, 2: 0, 3: 1, 4: 0, 5: 1}[i]
        self.sends(6 + 2 * (d - 1) + half).start()
        self.sends(12 + 2 * (d - 1) + half).start()

    def along_x(self, i):
        self.got(i)
        self.sends(i + 12).start()

    def sibling(self):
        for i in range(12, 24):
            self.got(i)

    def sent(self):
        for i in range(24):
            self.sends(i).wait_send()


Y_ROUNDS = ((0, 3), (1, 4), (2, 5))
X_ROUNDS = ((10, 7), (11, 6), (8, 9))
PIECE = 16


def spread_rows(row):
    return jnp.transpose(jnp.broadcast_to(row, (128, row.shape[1])))


def count(flags):
    return jnp.sum(jnp.where(flags, 1.0, 0.0), axis=0, keepdims=True)


def describe(seg_ids, seg_doc, doc_lens, y):
    lane = lax.broadcasted_iota(jnp.int32, (1, 128), 1)

    def window(n):
        return seg_ids[:, pl.ds(pl.multiple_of(128 * jnp.maximum(n, 0), 128), 128)].astype(F32)

    own = [window(SIDE * s + y) for s in range(SIDE)]
    own_at = [(128 * (SIDE * s + y) + lane).astype(F32) for s in range(SIDE)]
    halo, halo_at = [], []
    for s in (0, 2):
        low, high = window(SIDE * s + y - 1), window(SIDE * (s + 1) + y - 1)
        both = jnp.where(lane < HALO, pltpu.roll(low, HALO, 1), high)
        start = jnp.where(
            lane < HALO, 128 * (SIDE * s + y) - HALO, 128 * (SIDE * (s + 1) + y) - 2 * HALO
        )
        at = (start + lane).astype(F32)
        halo.append(jnp.where(at < 0.0, -1.0, both))
        halo_at.append(at)
    seg = jnp.concatenate(own + halo, axis=1)
    at = jnp.concatenate(own_at + halo_at, axis=1)
    keys = seg.shape[1]
    tokens = SIDE * 128
    number = lax.broadcasted_iota(jnp.int32, (128, keys), 0).astype(F32)
    docs = spread_rows(seg_doc[...].astype(F32))
    docs = jnp.concatenate([docs] * (keys // 128), axis=1)
    doc = jnp.sum(jnp.where(number == seg, docs, 0.0), axis=0, keepdims=True)
    order = jnp.where(seg < 0.0, 65536.0 + at, doc * 2048.0 + at)
    tall, tall_seg = spread_rows(order), spread_rows(seg)
    key_rank, rank, pos = [], [], []
    for c in range(keys // 128):
        cut = slice(128 * c, 128 * (c + 1))
        less = tall < order[:, cut]
        key_rank.append(count(less))
        if c < SIDE:
            rank.append(count(less[:tokens]))
            pos.append(count(less & (tall_seg == seg[:, cut])))
    key_rank, rank, pos = [jnp.concatenate(v, axis=1) for v in (key_rank, rank, pos)]
    doc = doc[:, :tokens]
    low, high = jnp.zeros_like(doc), jnp.zeros_like(doc)
    for d in range(doc_lens.shape[0]):
        length = doc_lens[d].astype(F32)
        low = low + jnp.where(doc > d, length, 0.0)
        high = high + jnp.where(doc >= d, length, 0.0)
    mine = key_rank[:, :tokens]
    ranges = [low, high, mine - pos, mine + 1.0]
    coarse = [jnp.floor(v * (1.0 / 64.0)) for v in ranges]
    fine = [v - 64.0 * c for v, c in zip(ranges, coarse)]
    table = jnp.concatenate(coarse + fine + [rank] * 8, axis=0)
    return table, jnp.concatenate([key_rank] * 8, axis=0), pos


def gather_project(
    hid, gain, inverse, seg_ids, seg_doc, doc_lens, wq, wkv, pfx, wo,
    q_out, kv, pfx_all, wo_all, table, key_table,
    xs, wqs, wkvs, cos, sin, send, recv, x_send, x_recv, halo_send, halo_recv, stay,
):
    x, core, z, y = place()
    here = lambda dx, dcore, dz, dy: device(
        x + dx, core if dcore == 0 else 1 - core, z + dz, y + dy
    )
    down = SIDE - 1
    stays = [
        pltpu.make_async_copy(own, every.at[y], stay.at[k])
        for k, (own, every) in enumerate([(wkv, wkvs), (wq, wqs), (pfx, pfx_all), (wo, wo_all)])
    ]
    for copy in stays:
        copy.start()
    greet([
        here(0, 0, 0, 1), here(0, 0, 0, down), here(0, 0, 1, 0), here(0, 0, down, 0),
        here(1, 0, 0, 0), here(down, 0, 0, 0), here(0, 1, 0, 0),
    ])

    def pieces(own, every, step, size, offset=0, cols=None):
        across = slice(None) if cols is None else pl.ds(*cols)

        def at(n):
            return pl.ds(pl.multiple_of(n * step + offset, size), size)

        return lambda n: own.at[at(n), across], lambda s, n: every.at[s, at(n), across]

    parts = [
        pieces(wkv, wkvs, 512, 512),
        pieces(wq, wqs, 512, 256),
        pieces(wq, wqs, 512, 256, 256),
        pieces(pfx, pfx_all, 512, 512),
        pieces(wo, wo_all, 32, 32, 0, (0, 2048)),
        pieces(wo, wo_all, 32, 32, 0, (2048, 2048)),
    ]
    units = [Spread(own, every, send.at[k], recv.at[k]) for k, (own, every) in enumerate(parts)]
    units[0].start()

    values = hid[...].astype(F32)
    scale = lax.rsqrt(jnp.mean(values * values, axis=-1, keepdims=True) + EPS)
    xs[z] = (values * scale * gain[...].astype(F32)).astype(BF16)

    per_half = HALO // PIECE

    def x_copy(side, n, d=0):
        view = xs.at[(z + d) % SIDE, pl.ds(PIECE * n, PIECE), :]
        i = n + (2 * per_half if d else 0)
        to = here(0, 0, down if side else 1, 0)
        return remote(view, view, x_send.at[side, i], x_recv.at[side, i], to)

    def first_half(side, k):
        return (k + per_half * side) % (2 * per_half)

    def x_own(k):
        if k < 2 * per_half:
            for side in range(2):
                x_copy(side, first_half(side, k)).start()

    def x_got(k):
        for side in range(2):
            d = 1 if side else down
            if k < 2 * per_half:
                n = first_half(side, k)
                view = xs.at[(z + d) % SIDE, pl.ds(PIECE * n, PIECE), :]
                i = n
            else:
                n = first_half(side, k - 2 * per_half)
                view = xs.at[(z + 2) % SIDE, pl.ds(PIECE * n, PIECE), :]
                i = n + 2 * per_half
            remote(view, view, x_send.at[side, i], x_recv.at[side, i], here(0, 0, 1, 0)).wait_recv()
            if k < per_half:
                x_copy(side, n, d).start()

    tokens = SIDE * 128
    half_rows = 2 * 128

    def project_kv():
        for s in range(SIDE):
            @pl.loop(0, 2)
            def _(m):
                tall = pl.ds(pl.multiple_of(m * half_rows, half_rows), half_rows)
                lhs = xs[pl.ds(2 * m, 2)].reshape(half_rows, xs.shape[2])
                got = jnp.dot(lhs, wkvs[s], preferred_element_type=F32)
                if s % 2 == 0:
                    got = rotate(got, cos[tall, :], sin[tall, :])
                kv[tall, pl.ds(HEAD * s, HEAD)] = got.astype(BF16)

    def project_q(s):
        @pl.loop(0, 2)
        def _(m):
            tall = pl.ds(pl.multiple_of(m * half_rows, half_rows), half_rows)
            lhs = xs[pl.ds(2 * m, 2)].reshape(half_rows, xs.shape[2])
            got = jnp.dot(lhs, wqs[s], preferred_element_type=F32)
            for n in range(2):
                one = rotate(got[:, HEAD * n : HEAD * (n + 1)], cos[tall, :], sin[tall, :])
                q_out[tall, pl.ds(HEAD * (2 * s + n), HEAD)] = one.astype(BF16)

    def halo_copy(slot):
        dst = (slot + y // 3) % SIDE
        return remote(
            kv.at[pl.ds(128 * slot + HALO, HALO), :],
            kv.at[pl.ds(pl.multiple_of(tokens + HALO * dst, HALO), HALO), :],
            halo_send.at[slot],
            halo_recv.at[slot],
            here(0, 0, 0, 1),
        )

    def describe_tokens():
        rows, key_rows, pos = describe(seg_ids, seg_doc, doc_lens, y)
        table[...] = rows
        key_table[...] = key_rows
        angle = (pfx.shape[0] + spread_rows(pos)) * inverse[...]
        cos[...] = jnp.cos(angle)
        lane = lax.broadcasted_iota(jnp.int32, angle.shape, 1)
        turn = jnp.sin(angle)
        sin[...] = jnp.where(lane < HEAD // 2, -turn, turn)

    def keys_and_values():
        for k in range(2):
            stays[k].wait()
        for unit in units[:3]:
            unit.sibling()
        project_kv()
        for slot in range(SIDE):
            halo_copy(slot).start()

    extra = {3: describe_tokens, 12: keys_and_values}
    for s in range(SIDE):
        extra[13 + s] = functools.partial(project_q, s)
    lag = 2
    ahead = 3
    for k in range(ahead):
        x_own(k)
    for t in range(3 * len(units) + lag):
        if t < 3 * len(units):
            for i in Y_ROUNDS[t % 3]:
                units[t // 3].along_y(i)
            if t % 3 == 0 and t // 3 + 1 < len(units):
                units[t // 3 + 1].start()
        if t < 3 * per_half:
            x_got(t)
            x_own(t + ahead)
        if t >= lag:
            for i in X_ROUNDS[(t - lag) % 3]:
                units[(t - lag) // 3].along_x(i)
        if t in extra:
            extra[t]()
    for unit in units[3:]:
        unit.sibling()
    for k in range(2, 4):
        stays[k].wait()
    for slot in range(SIDE):
        halo_copy(slot).wait()
    for side in range(2):
        for n in range(2 * per_half):
            x_copy(side, n).wait_send()
        for k in range(per_half):
            x_copy(side, first_half(side, k), 1 if side else down).wait_send()
    for unit in units:
        unit.sent()


def attend(table, key_table, q, kv, pfx, out, perm, qs, kvs, ranges, outs, top, total, acc):
    tokens, news, prefix = q.shape[0], kv.shape[0], pfx.shape[1]
    tile, keys, group = 64, 256, 4
    lanes = group * tile
    exponent = math.log2(math.e) / math.sqrt(HEAD)

    def one_hot(flags):
        return jnp.where(flags, 1.0, 0.0).astype(BF16)

    rank = table[8:9, :]
    spots = lax.broadcasted_iota(jnp.int32, (tokens, tokens), 0).astype(F32)
    qs[...] = jnp.dot(one_hot(spots == rank), q[...], preferred_element_type=F32).astype(BF16)
    spots = lax.broadcasted_iota(jnp.int32, (news, news), 0).astype(F32)
    kvs[...] = jnp.dot(
        one_hot(spots == key_table[0:1, :]), kv[...], preferred_element_type=F32
    ).astype(BF16)
    tall = spread_rows(rank)
    lane = lax.broadcasted_iota(jnp.int32, (tokens, 128), 1)
    rows = table[...].astype(BF16)
    for i in range(tokens // tile):
        flags = one_hot(tall == ((lane % tile) + tile * i).astype(F32))
        got = jnp.dot(rows, flags, preferred_element_type=F32)
        got = 64.0 * got[0:8] + jnp.concatenate([got[4:8]] * 2, axis=0)
        ranges[i] = jnp.concatenate([got] * (lanes // 128), axis=1)
    for c in range(tokens // 128):
        perm[:, pl.ds(128 * c, 128)] = one_hot(tall == (lane + 128 * c).astype(F32))

    @pl.loop(0, tokens // tile)
    def _(i):
        cut = pl.ds(pl.multiple_of(i * tile, tile), tile)
        top[...] = jnp.full(top.shape, MASKED, F32)
        total[...] = jnp.zeros(total.shape, F32)
        acc[...] = jnp.zeros(acc.shape, F32)
        queries = [
            jnp.concatenate(
                [qs[cut, pl.ds(HEAD * (group * h + n), HEAD)] for n in range(group)], axis=0
            )
            for h in range(2)
        ]

        def sweep(low, high, size, load):
            first = jnp.min(low).astype(jnp.int32) // 128 * 128
            last = jnp.max(high).astype(jnp.int32)

            @pl.loop(0, (last - first + keys - 1) // keys)
            def _(j):
                begin = first + j * keys
                start = pl.multiple_of(jnp.minimum(begin, size - keys), 128)
                at = lax.broadcasted_iota(jnp.int32, (keys, lanes), 0)
                near = jnp.maximum(low.astype(jnp.int32), begin) - start
                far = high.astype(jnp.int32) - start
                allowed = (at >= near) & (at < far)
                for h in range(2):
                    key, value = load(h, pl.ds(start, keys))
                    s = lax.dot_general(
                        key, queries[h], (((1,), (1,)), ((), ())), preferred_element_type=F32
                    )
                    s = jnp.where(allowed, s * exponent, MASKED)
                    old = top[h, 0:1, :]
                    new = jnp.maximum(old, jnp.max(s, axis=0, keepdims=True))
                    p = jnp.exp2(s - new)
                    fade = jnp.exp2(old - new)
                    top[h, 0:1, :] = new
                    total[h, 0:1, :] = total[h, 0:1, :] * fade + jnp.sum(p, axis=0, keepdims=True)
                    acc[h] = acc[h] * fade + lax.dot_general(
                        value, p.astype(BF16), (((0,), (0,)), ((), ())), preferred_element_type=F32
                    )

        got = ranges[i]
        sweep(
            got[2:3],
            got[3:4],
            news,
            lambda h, at: (
                kvs[at, pl.ds(2 * HEAD * h, HEAD)],
                kvs[at, pl.ds(2 * HEAD * h + HEAD, HEAD)],
            ),
        )
        sweep(got[0:1], got[1:2], prefix, lambda h, at: (pfx[2 * h, at, :], pfx[2 * h + 1, at, :]))
        for h in range(2):
            done = jnp.transpose(acc[h] / total[h, 0:1, :]).astype(BF16)
            for n in range(group):
                outs[cut, pl.ds(HEAD * (group * h + n), HEAD)] = done[n * tile : (n + 1) * tile]

    out[...] = jnp.dot(perm[...], outs[...], preferred_element_type=F32).astype(BF16)


COLS = 512


def project_reduce(
    att, wo, hid, mixed,
    far_out, near_out, far_in, near_in, far_send, far_recv, near_send, near_recv,
):
    x, core, z, y = place()
    sides = [device(x, core, z + 1, y), device(x, core, z + SIDE - 1, y)]
    greet(sides)
    chunks = wo.shape[1] // COLS

    def partial(slot, j):
        return jnp.dot(
            att[slot % SIDE], wo[:, pl.ds(COLS * j, COLS)], preferred_element_type=F32
        )

    def far(j):
        return remote(
            far_out.at[j], far_in.at[j], far_send.at[j], far_recv.at[j], sides[j % 2]
        )

    def near(side, j):
        return remote(
            near_out.at[side, j],
            near_in.at[side, j],
            near_send.at[side, j],
            near_recv.at[side, j],
            sides[side],
        )

    for j in range(chunks):
        far_out[j] = partial(z + 2, j).astype(BF16)
        far(j).start()
    for j in range(chunks):
        side = 1 - j % 2
        near_out[side, j] = partial(z + (3 if side else 1), j).astype(BF16)
        near(side, j).start()
        side = j % 2
        mine = partial(z + (3 if side else 1), j)
        far(j).wait_recv()
        near_out[side, j] = (mine + far_in[j].astype(F32)).astype(BF16)
        near(side, j).start()
    for j in range(chunks):
        cut = pl.ds(COLS * j, COLS)
        mine = partial(z, j) + hid[:, cut].astype(F32)
        near(0, j).wait_recv()
        near(1, j).wait_recv()
        mine = mine + near_in[0, j].astype(F32) + near_in[1, j].astype(F32)
        mixed[:, cut] = mine.astype(BF16)
    for j in range(chunks):
        far(j).wait_send()
        near(0, j).wait_send()
        near(1, j).wait_send()


def local(hidden_in, norm_gain, w_query, keyvalue_weight, w_out, cache, seg_ids, seg_doc, doc_lens):
    prefix_len = cache.shape[0]
    width = hidden_in.shape[1]
    inverse = THETA ** (-(np.arange(HEAD // 2, dtype=np.float64) * 2.0 / HEAD))
    inverse = jnp.asarray(np.concatenate([inverse, inverse])[None, :], F32)

    vmem = pl.BlockSpec(memory_space=pltpu.VMEM)
    smem = pl.BlockSpec(memory_space=pltpu.SMEM)
    whole = pl.BlockSpec(memory_space=pl.ANY)
    tokens = SIDE * 128
    news = tokens + SIDE * HALO
    q, kv, pfx, wo, table, key_table = pl.pallas_call(
        gather_project,
        out_shape=(
            jax.ShapeDtypeStruct((tokens, 8 * HEAD), BF16),
            jax.ShapeDtypeStruct((news, 4 * HEAD), BF16),
            jax.ShapeDtypeStruct((SIDE, prefix_len, HEAD), BF16),
            jax.ShapeDtypeStruct((SIDE,) + w_out.shape, BF16),
            jax.ShapeDtypeStruct((16, tokens), F32),
            jax.ShapeDtypeStruct((8, news), F32),
        ),
        in_specs=[vmem] * 5 + [smem] + [whole] * 4,
        out_specs=(vmem,) * 6,
        scratch_shapes=[
            pltpu.VMEM((SIDE, 128, width), BF16),
            pltpu.VMEM((SIDE,) + w_query.shape, BF16),
            pltpu.VMEM((SIDE,) + keyvalue_weight.shape, BF16),
            pltpu.VMEM((tokens, HEAD), F32),
            pltpu.VMEM((tokens, HEAD), F32),
            pltpu.SemaphoreType.DMA((6, 24)),
            pltpu.SemaphoreType.DMA((6, 24)),
            pltpu.SemaphoreType.DMA((2, 16)),
            pltpu.SemaphoreType.DMA((2, 16)),
            pltpu.SemaphoreType.DMA((4,)),
            pltpu.SemaphoreType.DMA((4,)),
            pltpu.SemaphoreType.DMA((4,)),
        ],
        compiler_params=pltpu.CompilerParams(
            collective_id=0, has_side_effects=True, vmem_limit_bytes=36 * 2**20
        ),
        name="gather_project",
    )(
        hidden_in,
        norm_gain[None, :],
        inverse,
        seg_ids[None, :],
        seg_doc[None, :],
        doc_lens,
        w_query,
        keyvalue_weight,
        cache,
        w_out,
    )

    attended = pl.pallas_call(
        attend,
        out_shape=jax.ShapeDtypeStruct((tokens, 8 * HEAD), BF16),
        in_specs=[vmem] * 5,
        out_specs=vmem,
        scratch_shapes=[
            pltpu.VMEM((tokens, tokens), BF16),
            pltpu.VMEM((tokens, 8 * HEAD), BF16),
            pltpu.VMEM((news, 4 * HEAD), BF16),
            pltpu.VMEM((8, 8, 256), F32),
            pltpu.VMEM((tokens, 8 * HEAD), BF16),
            pltpu.VMEM((2, 8, 256), F32),
            pltpu.VMEM((2, 8, 256), F32),
            pltpu.VMEM((2, HEAD, 256), F32),
        ],
        compiler_params=pltpu.CompilerParams(vmem_limit_bytes=32 * 2**20),
        name="attend",
    )(table, key_table, q, kv, pfx)

    chunks = width // COLS
    return pl.pallas_call(
        project_reduce,
        out_shape=jax.ShapeDtypeStruct(hidden_in.shape, BF16),
        in_specs=[vmem] * 3,
        out_specs=vmem,
        scratch_shapes=[
            pltpu.VMEM((chunks, 128, COLS), BF16),
            pltpu.VMEM((2, chunks, 128, COLS), BF16),
            pltpu.VMEM((chunks, 128, COLS), BF16),
            pltpu.VMEM((2, chunks, 128, COLS), BF16),
            pltpu.SemaphoreType.DMA((chunks,)),
            pltpu.SemaphoreType.DMA((chunks,)),
            pltpu.SemaphoreType.DMA((2, chunks)),
            pltpu.SemaphoreType.DMA((2, chunks)),
        ],
        compiler_params=pltpu.CompilerParams(
            collective_id=1, has_side_effects=True, vmem_limit_bytes=32 * 2**20
        ),
        name="project_reduce",
    )(attended.reshape(SIDE, 128, 8 * HEAD), wo.reshape(-1, width), hidden_in)


def solution(mesh):
    return jax.shard_map(
        local,
        mesh=mesh,
        in_specs=(
            P(("dp", "tensor"), None),
            P(),
            P(None, "tensor"),
            P(None, "tensor"),
            P("tensor", None),
            P(None, "tensor"),
            P("dp"),
            P("dp"),
            P(),
        ),
        out_specs=P(("dp", "tensor"), None),
        check_vma=False,
    )
```

time: 224 us -> 170 us (0.76)
  Pallas kernels: 203 us -> 155 us
  other arithmetic: 6.41 us -> 0 us
    pallas_call x1, Pallas kernels: 84.2 us -> 32.5 us  [local(): pl.pallas_call(attend, out_shape=jax.ShapeDtypeStruct((tokens, 8 * HEAD),...]
    reduce_sum x8 -> x0, other arithmetic: 4.69 us -> none  [the longest x1 1.45 us: tables(): jnp.sum((seg_ids[None, :] < key_seg[:, None]).astype(jnp.int32), axis=1)]
    pallas_call x1, Pallas kernels: 33.6 us -> 37.6 us  [local(): pl.pallas_call(project_reduce, out_shape=jax.ShapeDtypeStruct(hidden_in.s...]
    unnamed x13 -> x23, local copies, waits for them, and re-layouts: 10.2 us -> 13.9 us
where the time goes in v2:
time: 170 us
  Pallas kernels  155 us (91%)
  local copies, waits for them, and re-layouts  14.6 us (9%)
    pallas_call x1, Pallas kernels, local(): pl.pallas_call(gather_project, out_shape=(jax.ShapeDtypeStruct((tokens, 8...  85.2 us
    pallas_call x1, Pallas kernels, local(): pl.pallas_call(project_reduce, out_shape=jax.ShapeDtypeStruct(hidden_in.s...  37.6 us
    pallas_call x1, Pallas kernels, local(): pl.pallas_call(attend, out_shape=jax.ShapeDtypeStruct((tokens, 8 * HEAD),...  32.5 us
    unnamed x23, local copies, waits for them, and re-layouts  13.9 us

profile of v2, /device:TPU:0, one launch (start us, length us, event | category | flops | bytes accessed | tf_op | source)
XLA Modules:
  0.0 169.9 jit_solution(9201783720484703020)
XLA Ops:
  0.0 0.7 broadcast_in_dim.9.gain
  0.7 0.0 copy-start.1
  0.7 1.2 copy-done.1
  1.9 0.0 copy-start.3
  1.9 1.6 copy-done.3
  3.5 0.0 copy-start.4
  3.5 1.6 copy-done.4
  5.1 0.0 copy-start.5
  5.1 1.2 copy-done.5
  6.3 0.0 copy-start.6
  6.3 1.2 copy-done.6
  7.6 0.0 copy-start.7
  7.6 0.7 copy-done.7
  8.3 0.0 copy-start.8
  8.3 0.7 copy-done.8
  8.9 0.0 copy-start.9
  8.9 0.7 copy-done.9
  9.6 0.0 copy-start.10
  9.6 0.7 copy-done.10
  10.2 85.2 %gather_project.1 = (bf16[512,1024]{1,0:T(8,128)(2,1)S(1)}, bf16[768,512]{1,0:T(8,128)(2,1)S(1)}, bf16[4,4096,128]{2,1,0:T(8,128)(2,1)S(1)}, bf16[4,256,4096]{2,...) custom-call(bf16[128,4096]{1,0:T(8,128)(2,1)S(1)} %copy-done.1, ...), custom_call_target="tpu_custom_call" | custom-call | tf_op jit(solution)/shard_map/gather_project/pallas_call | solution.py:510
  95.5 0.0 copy-start.2
  95.5 32.5 %attend.1 = bf16[512,1024]{1,0:T(8,128)(2,1)S(1)} custom-call(f32[16,512]{1,0:T(8,128)S(1)} %get-tuple-element.11.table, f32[8,768]{1,0:T(8,128)S(1)} %get-tuple-element.12.key_table, bf16[512,1024]{1,0:T(8,128)(2,1)S(1)} %get-tuple-element.13.q, bf16[768,512]{1,0:T(8,128)(2,1)S(1)} %get-tuple-element.14.kv, bf16[4,4096,128]{2,1,0:T(8,128)(2,1)S(1)} %get-tuple-element.15.pfx), custom_call_target="tpu_custom_call" | custom-call | tf_op jit(solution)/shard_map/attend/pallas_call | solution.py:553
  128.0 0.0 copy-done.2
  128.0 0.0 copy-start
  128.0 3.4 %copy-done = bf16[4,256,4096]{2,1,0:T(8,128)(2,1)S(1)} copy-done((bf16[4,256,4096]{2,1,0:T(8,128)(2,1)S(1)}, bf16[4,256,4096]{2,1,0:T(8,128)(2,1)}, u32[]{:S(2)}) %copy-start) | copy-done | bytes 8388632
  131.4 37.6 %project_reduce.1 = bf16[128,4096]{1,0:T(8,128)(2,1)S(1)} custom-call(bf16[4,128,1024]{2,1,0:T(8,128)(2,1)S(1)} %bitcast.5, bf16[1024,4096]{1,0:T(8,128)(2,1)S(1)} %bitcast.4, bf16[128,4096]{1,0:T(8,128)(2,1)S(1)} %copy-done.2), custom_call_target="tpu_custom_call" | custom-call | tf_op jit(solution)/shard_map/project_reduce/pallas_call | solution.py:573
  169.0 1.0 copy.12
Async XLA Ops:
  0.7 1.2 copy-start.1
  1.9 1.6 copy-start.3
  3.5 1.6 copy-start.4
  5.1 1.2 copy-start.5
  6.3 1.2 copy-start.6
  7.6 0.7 copy-start.7
  8.3 0.7 copy-start.8
  8.9 0.7 copy-start.9
  9.6 0.7 copy-start.10
  95.5 32.5 %copy-start.2 = (bf16[128,4096]{1,0:T(8,128)(2,1)S(1)}, bf16[128,4096]{1,0:T(8,128)(2,1)}, u32[]{:S(2)}) copy-start(bf16[128,4096]{1,0:T(8,128)(2,1)} %hid.3) | copy-start | bytes 3145732
  128.0 3.4 %copy-start = (bf16[4,256,4096]{2,1,0:T(8,128)(2,1)S(1)}, bf16[4,256,4096]{2,1,0:T(8,128)(2,1)}, u32[]{:S(2)}) copy-start(bf16[4,256,4096]{2,1,0:T(8,128)(2,1)} %get-tuple-element.16) | copy-start | bytes 25165828

commit v3 on v2

--- a/solution.py
+++ b/solution.py
@@ -3,7 +3,6 @@
 
 import jax
 import jax.numpy as jnp
-import numpy as np
 from jax import lax
 from jax.experimental import pallas as pl
 from jax.experimental.pallas import tpu as pltpu
@@ -46,9 +45,18 @@
     return v * cos + pltpu.roll(v, HEAD // 2, 1) * sin
 
 
+def pieces(own, every, step, size, offset=0, cols=None):
+    across = slice(None) if cols is None else pl.ds(*cols)
+
+    def at(n):
+        return pl.ds(pl.multiple_of(n * step + offset, size), size)
+
+    return lambda n: own.at[at(n), across], lambda s, n: every.at[s, at(n), :]
+
+
 class Spread:
-    def __init__(self, own, block, send, recv):
-        self.own, self.block, self.send, self.recv = own, block, send, recv
+    def __init__(self, own, block, bulk, send, recv):
+        self.own, self.block, self.bulk, self.send, self.recv = own, block, bulk, send, recv
         self.x, self.core, self.z, self.y = place()
 
     def number(self, parity, core, half):
@@ -61,7 +69,7 @@
         slot = (self.y + d + SIDE) % SIDE
         src = self.own(piece) if first else self.block(slot, piece)
         return remote(
-            src, self.block(slot, piece), self.send.at[i], self.recv.at[i], device(*to)
+            src, self.block(slot, piece), self.send, self.recv.at[min(i, 12)], device(*to)
         )
 
     def mine(self, half):
@@ -91,11 +99,9 @@
             piece = self.mine(half)
         else:
             d, half = 1 + (i % 6) // 2, i % 2
-            parity = self.x % 2 if 12 <= i < 18 else 1 - self.x % 2
-            core = self.core if i < 12 else 1 - self.core
-            piece = self.number(parity, core, half)
+            piece = self.number(1 - self.x % 2, self.core, half)
         view = self.block((self.y + d) % SIDE, piece)
-        remote(view, view, self.send.at[i], self.recv.at[i], device(*self.up(1))).wait_recv()
+        remote(view, view, self.send, self.recv.at[i], device(*self.up(1))).wait_recv()
 
     def start(self):
         for i in (0, 3, 1, 4):
@@ -117,12 +123,12 @@
         self.sends(i + 12).start()
 
     def sibling(self):
-        for i in range(12, 24):
-            self.got(i)
+        view = self.bulk(1)
+        remote(view, view, self.send, self.recv.at[12], device(*self.up(1))).wait_recv()
 
     def sent(self):
-        for i in range(24):
-            self.sends(i).wait_send()
+        view = self.bulk(2)
+        remote(view, view, self.send, self.recv.at[12], device(*self.up(1))).wait_send()
 
 
 Y_ROUNDS = ((0, 3), (1, 4), (2, 5))
@@ -190,9 +196,10 @@
 
 
 def gather_project(
-    hid, gain, inverse, seg_ids, seg_doc, doc_lens, wq, wkv, pfx, wo,
-    q_out, kv, pfx_all, wo_all, table, key_table,
-    xs, wqs, wkvs, cos, sin, send, recv, x_send, x_recv, halo_send, halo_recv, stay,
+    gain, hid_far, seg_ids_far, seg_doc_far, doc_lens_far, wq, wkv, pfx, wo,
+    q_out, kv, pfx_all, wo_low, table, key_table,
+    xs, wqs, wkvs, cos, sin, hid, seg_ids, seg_doc, doc_lens,
+    send, recv, x_send, x_recv, halo_send, halo_recv, stay,
 ):
     x, core, z, y = place()
     here = lambda dx, dcore, dz, dy: device(
@@ -200,8 +207,19 @@
     )
     down = SIDE - 1
     stays = [
-        pltpu.make_async_copy(own, every.at[y], stay.at[k])
-        for k, (own, every) in enumerate([(wkv, wkvs), (wq, wqs), (pfx, pfx_all), (wo, wo_all)])
+        pltpu.make_async_copy(src, dst, stay.at[k])
+        for k, (src, dst) in enumerate(
+            [
+                (hid_far, hid),
+                (seg_ids_far, seg_ids),
+                (seg_doc_far, seg_doc),
+                (doc_lens_far, doc_lens),
+                (wkv, wkvs.at[y]),
+                (wq, wqs.at[y]),
+                (pfx, pfx_all.at[y]),
+                (wo.at[:, pl.ds(0, wo_low.shape[2])], wo_low.at[y]),
+            ]
+        )
     ]
     for copy in stays:
         copy.start()
@@ -210,25 +228,20 @@
         here(1, 0, 0, 0), here(down, 0, 0, 0), here(0, 1, 0, 0),
     ])
 
-    def pieces(own, every, step, size, offset=0, cols=None):
-        across = slice(None) if cols is None else pl.ds(*cols)
-
-        def at(n):
-            return pl.ds(pl.multiple_of(n * step + offset, size), size)
-
-        return lambda n: own.at[at(n), across], lambda s, n: every.at[s, at(n), across]
+    def third(array, size):
+        return lambda n: array.at[pl.ds(0, 3), pl.ds(0, n * size), :]
 
     parts = [
-        pieces(wkv, wkvs, 512, 512),
-        pieces(wq, wqs, 512, 256),
-        pieces(wq, wqs, 512, 256, 256),
-        pieces(pfx, pfx_all, 512, 512),
-        pieces(wo, wo_all, 32, 32, 0, (0, 2048)),
-        pieces(wo, wo_all, 32, 32, 0, (2048, 2048)),
+        pieces(wkv, wkvs, 512, 512) + (third(wkvs, 2048),),
+        pieces(wq, wqs, 512, 256) + (third(wqs, 1024),),
+        pieces(wq, wqs, 512, 256, 256) + (third(wqs, 1024),),
+        pieces(pfx, pfx_all, 512, 512) + (third(pfx_all, 2048),),
+        pieces(wo, wo_low, 32, 32, 0, (0, wo_low.shape[2])) + (third(wo_low, 128),),
     ]
-    units = [Spread(own, every, send.at[k], recv.at[k]) for k, (own, every) in enumerate(parts)]
+    units = [Spread(*part, send.at[k], recv.at[k]) for k, part in enumerate(parts)]
     units[0].start()
 
+    stays[0].wait()
     values = hid[...].astype(F32)
     scale = lax.rsqrt(jnp.mean(values * values, axis=-1, keepdims=True) + EPS)
     xs[z] = (values * scale * gain[...].astype(F32)).astype(BF16)
@@ -239,7 +252,7 @@
         view = xs.at[(z + d) % SIDE, pl.ds(PIECE * n, PIECE), :]
         i = n + (2 * per_half if d else 0)
         to = here(0, 0, down if side else 1, 0)
-        return remote(view, view, x_send.at[side, i], x_recv.at[side, i], to)
+        return remote(view, view, x_send.at[side], x_recv.at[side, i], to)
 
     def first_half(side, k):
         return (k + per_half * side) % (2 * per_half)
@@ -260,7 +273,7 @@
                 n = first_half(side, k - 2 * per_half)
                 view = xs.at[(z + 2) % SIDE, pl.ds(PIECE * n, PIECE), :]
                 i = n + 2 * per_half
-            remote(view, view, x_send.at[side, i], x_recv.at[side, i], here(0, 0, 1, 0)).wait_recv()
+            remote(view, view, x_send.at[side], x_recv.at[side, i], here(0, 0, 1, 0)).wait_recv()
             if k < per_half:
                 x_copy(side, n, d).start()
 
@@ -299,17 +312,22 @@
         )
 
     def describe_tokens():
+        for k in range(1, 4):
+            stays[k].wait()
         rows, key_rows, pos = describe(seg_ids, seg_doc, doc_lens, y)
         table[...] = rows
         key_table[...] = key_rows
-        angle = (pfx.shape[0] + spread_rows(pos)) * inverse[...]
+        lane = lax.broadcasted_iota(jnp.int32, (1, HEAD), 1)
+        inverse = jnp.zeros((1, HEAD), F32)
+        for i in range(HEAD // 2):
+            inverse = jnp.where(lane % (HEAD // 2) == i, THETA ** (-2.0 * i / HEAD), inverse)
+        angle = (pfx.shape[0] + spread_rows(pos)) * inverse
         cos[...] = jnp.cos(angle)
-        lane = lax.broadcasted_iota(jnp.int32, angle.shape, 1)
         turn = jnp.sin(angle)
         sin[...] = jnp.where(lane < HEAD // 2, -turn, turn)
 
     def keys_and_values():
-        for k in range(2):
+        for k in range(4, 6):
             stays[k].wait()
         for unit in units[:3]:
             unit.sibling()
@@ -340,15 +358,13 @@
             extra[t]()
     for unit in units[3:]:
         unit.sibling()
-    for k in range(2, 4):
+    for k in range(6, 8):
         stays[k].wait()
     for slot in range(SIDE):
         halo_copy(slot).wait()
     for side in range(2):
-        for n in range(2 * per_half):
-            x_copy(side, n).wait_send()
-        for k in range(per_half):
-            x_copy(side, first_half(side, k), 1 if side else down).wait_send()
+        view = xs.at[pl.ds(0, 3), pl.ds(0, HALO), :]
+        remote(view, view, x_send.at[side], x_recv.at[side, 0], here(0, 0, 1, 0)).wait_send()
     for unit in units:
         unit.sent()
 
@@ -444,23 +460,37 @@
 
 
 def project_reduce(
-    att, wo, hid, mixed,
-    far_out, near_out, far_in, near_in, far_send, far_recv, near_send, near_recv,
+    att, wo_low, wo, hid_far, mixed,
+    wo_high, hid, far_out, near_out, far_in, near_in,
+    far_send, far_recv, near_send, near_recv, send, recv, stay,
 ):
     x, core, z, y = place()
-    sides = [device(x, core, z + 1, y), device(x, core, z + SIDE - 1, y)]
-    greet(sides)
-    chunks = wo.shape[1] // COLS
+    down = SIDE - 1
+    sides = [device(x, core, z + 1, y), device(x, core, z + down, y)]
+    half = wo_low.shape[2]
+    stays = [
+        pltpu.make_async_copy(wo.at[:, pl.ds(half, half)], wo_high.at[y], stay.at[0]),
+        pltpu.make_async_copy(hid_far, hid, stay.at[1]),
+    ]
+    for copy in stays:
+        copy.start()
+    greet(
+        sides
+        + [device(x, core, z, y + 1), device(x, core, z, y + down)]
+        + [device(x + 1, core, z, y), device(x + down, core, z, y), device(x, 1 - core, z, y)]
+    )
+    bulk = lambda n: wo_high.at[pl.ds(0, 3), pl.ds(0, 128 * n), :]
+    unit = Spread(*pieces(wo, wo_high, 32, 32, 0, (half, half)), bulk, send.at[0], recv.at[0])
+    unit.start()
+    chunks = 2 * half // COLS
 
     def partial(slot, j):
-        return jnp.dot(
-            att[slot % SIDE], wo[:, pl.ds(COLS * j, COLS)], preferred_element_type=F32
-        )
+        source, at = (wo_low, j) if j < chunks // 2 else (wo_high, j - chunks // 2)
+        weight = source[:, :, pl.ds(COLS * at, COLS)].reshape(-1, COLS)
+        return jnp.dot(att[slot % SIDE], weight, preferred_element_type=F32)
 
     def far(j):
-        return remote(
-            far_out.at[j], far_in.at[j], far_send.at[j], far_recv.at[j], sides[j % 2]
-        )
+        return remote(far_out.at[j], far_in.at[j], far_send.at[j], far_recv.at[j], sides[j % 2])
 
     def near(side, j):
         return remote(
@@ -471,18 +501,47 @@
             sides[side],
         )
 
-    for j in range(chunks):
+    def far_step(j):
         far_out[j] = partial(z + 2, j).astype(BF16)
         far(j).start()
-    for j in range(chunks):
+
+    def near_step(j):
         side = 1 - j % 2
-        near_out[side, j] = partial(z + (3 if side else 1), j).astype(BF16)
+        near_out[side, j] = partial(z + (down if side else 1), j).astype(BF16)
         near(side, j).start()
         side = j % 2
-        mine = partial(z + (3 if side else 1), j)
+        mine = partial(z + (down if side else 1), j)
         far(j).wait_recv()
         near_out[side, j] = (mine + far_in[j].astype(F32)).astype(BF16)
         near(side, j).start()
+
+    def along_y(r):
+        for i in Y_ROUNDS[r]:
+            unit.along_y(i)
+
+    def along_x(r):
+        for i in X_ROUNDS[r]:
+            unit.along_x(i)
+
+    for j in range(chunks // 2):
+        far_step(j)
+    along_y(0)
+    near_step(0)
+    near_step(1)
+    along_y(1)
+    along_x(0)
+    near_step(2)
+    along_y(2)
+    along_x(1)
+    near_step(3)
+    along_x(2)
+    stays[0].wait()
+    unit.sibling()
+    for j in range(chunks // 2, chunks):
+        far_step(j)
+    for j in range(chunks // 2, chunks):
+        near_step(j)
+    stays[1].wait()
     for j in range(chunks):
         cut = pl.ds(COLS * j, COLS)
         mine = partial(z, j) + hid[:, cut].astype(F32)
@@ -494,30 +553,29 @@
         far(j).wait_send()
         near(0, j).wait_send()
         near(1, j).wait_send()
+    unit.sent()
 
 
 def local(hidden_in, norm_gain, w_query, keyvalue_weight, w_out, cache, seg_ids, seg_doc, doc_lens):
     prefix_len = cache.shape[0]
     width = hidden_in.shape[1]
-    inverse = THETA ** (-(np.arange(HEAD // 2, dtype=np.float64) * 2.0 / HEAD))
-    inverse = jnp.asarray(np.concatenate([inverse, inverse])[None, :], F32)
-
+    half = width // 2
+    far = lambda array: pltpu.with_memory_space_constraint(array, pltpu.HBM)
     vmem = pl.BlockSpec(memory_space=pltpu.VMEM)
-    smem = pl.BlockSpec(memory_space=pltpu.SMEM)
-    whole = pl.BlockSpec(memory_space=pl.ANY)
+    whole = pl.BlockSpec(memory_space=pltpu.HBM)
     tokens = SIDE * 128
     news = tokens + SIDE * HALO
-    q, kv, pfx, wo, table, key_table = pl.pallas_call(
+    q, kv, pfx, wo_low, table, key_table = pl.pallas_call(
         gather_project,
         out_shape=(
             jax.ShapeDtypeStruct((tokens, 8 * HEAD), BF16),
             jax.ShapeDtypeStruct((news, 4 * HEAD), BF16),
             jax.ShapeDtypeStruct((SIDE, prefix_len, HEAD), BF16),
-            jax.ShapeDtypeStruct((SIDE,) + w_out.shape, BF16),
+            jax.ShapeDtypeStruct((SIDE, w_out.shape[0], half), BF16),
             jax.ShapeDtypeStruct((16, tokens), F32),
             jax.ShapeDtypeStruct((8, news), F32),
         ),
-        in_specs=[vmem] * 5 + [smem] + [whole] * 4,
+        in_specs=[vmem] + [whole] * 8,
         out_specs=(vmem,) * 6,
         scratch_shapes=[
             pltpu.VMEM((SIDE, 128, width), BF16),
@@ -525,29 +583,32 @@
             pltpu.VMEM((SIDE,) + keyvalue_weight.shape, BF16),
             pltpu.VMEM((tokens, HEAD), F32),
             pltpu.VMEM((tokens, HEAD), F32),
-            pltpu.SemaphoreType.DMA((6, 24)),
-            pltpu.SemaphoreType.DMA((6, 24)),
-            pltpu.SemaphoreType.DMA((2, 16)),
+            pltpu.VMEM(hidden_in.shape, BF16),
+            pltpu.VMEM((1,) + seg_ids.shape, jnp.int32),
+            pltpu.VMEM((1,) + seg_doc.shape, jnp.int32),
+            pltpu.SMEM(doc_lens.shape, jnp.int32),
+            pltpu.SemaphoreType.DMA((5,)),
+            pltpu.SemaphoreType.DMA((5, 13)),
+            pltpu.SemaphoreType.DMA((2,)),
             pltpu.SemaphoreType.DMA((2, 16)),
             pltpu.SemaphoreType.DMA((4,)),
             pltpu.SemaphoreType.DMA((4,)),
-            pltpu.SemaphoreType.DMA((4,)),
+            pltpu.SemaphoreType.DMA((8,)),
         ],
         compiler_params=pltpu.CompilerParams(
-            collective_id=0, has_side_effects=True, vmem_limit_bytes=36 * 2**20
+            collective_id=0, has_side_effects=True, vmem_limit_bytes=30 * 2**20
         ),
         name="gather_project",
     )(
-        hidden_in,
         norm_gain[None, :],
-        inverse,
-        seg_ids[None, :],
-        seg_doc[None, :],
-        doc_lens,
-        w_query,
-        keyvalue_weight,
-        cache,
-        w_out,
+        far(hidden_in),
+        far(seg_ids[None, :]),
+        far(seg_doc[None, :]),
+        far(doc_lens),
+        far(w_query),
+        far(keyvalue_weight),
+        far(cache),
+        far(w_out),
     )
 
     attended = pl.pallas_call(
@@ -573,9 +634,11 @@
     return pl.pallas_call(
         project_reduce,
         out_shape=jax.ShapeDtypeStruct(hidden_in.shape, BF16),
-        in_specs=[vmem] * 3,
+        in_specs=[vmem] * 2 + [whole] * 2,
         out_specs=vmem,
         scratch_shapes=[
+            pltpu.VMEM((SIDE, w_out.shape[0], half), BF16),
+            pltpu.VMEM(hidden_in.shape, BF16),
             pltpu.VMEM((chunks, 128, COLS), BF16),
             pltpu.VMEM((2, chunks, 128, COLS), BF16),
             pltpu.VMEM((chunks, 128, COLS), BF16),
@@ -584,12 +647,15 @@
             pltpu.SemaphoreType.DMA((chunks,)),
             pltpu.SemaphoreType.DMA((2, chunks)),
             pltpu.SemaphoreType.DMA((2, chunks)),
+            pltpu.SemaphoreType.DMA((1,)),
+            pltpu.SemaphoreType.DMA((1, 13)),
+            pltpu.SemaphoreType.DMA((2,)),
         ],
         compiler_params=pltpu.CompilerParams(
             collective_id=1, has_side_effects=True, vmem_limit_bytes=32 * 2**20
         ),
         name="project_reduce",
-    )(attended.reshape(SIDE, 128, 8 * HEAD), wo.reshape(-1, width), hidden_in)
+    )(attended.reshape(SIDE, 128, 8 * HEAD), wo_low, far(w_out), far(hidden_in))
 
 
 def solution(mesh):

time: 170 us -> 147 us (0.86)
  local copies, waits for them, and re-layouts: 14.6 us -> 1.68 us
  Pallas kernels: 155 us -> 144 us
    pallas_call x1, Pallas kernels: 85.2 us -> 69.8 us  [local(): pl.pallas_call(gather_project, out_shape=(jax.ShapeDtypeStruct((tokens, 8...]
    unnamed x23 -> x1, local copies, waits for them, and re-layouts: 13.9 us -> 0.97 us
    pallas_call x1, Pallas kernels: 37.6 us -> 44 us  [local(): pl.pallas_call(project_reduce, out_shape=jax.ShapeDtypeStruct(hidden_in.s...]
    pallas_call x1, Pallas kernels: 32.5 us -> 30.3 us  [local(): pl.pallas_call(attend, out_shape=jax.ShapeDtypeStruct((tokens, 8 * HEAD),...]
where the time goes in v3:
time: 147 us; the launch traced here: 146 us
  Pallas kernels  144 us (98%)
  local copies, waits for them, and re-layouts  1.68 us (1%)
    pallas_call x1, Pallas kernels, local(): pl.pallas_call(gather_project, out_shape=(jax.ShapeDtypeStruct((tokens, 8...  69.8 us
    pallas_call x1, Pallas kernels, local(): pl.pallas_call(project_reduce, out_shape=jax.ShapeDtypeStruct(hidden_in.s...  44 us
    pallas_call x1, Pallas kernels, local(): pl.pallas_call(attend, out_shape=jax.ShapeDtypeStruct((tokens, 8 * HEAD),...  30.3 us

profile of v3, /device:TPU:0, one launch (start us, length us, event | category | flops | bytes accessed | tf_op | source)
XLA Modules:
  0.0 145.8 jit_solution(16787152961155385675)
XLA Ops:
  0.0 0.7 broadcast_in_dim.9.gain
  0.7 69.8 %gather_project.1 = (bf16[512,1024]{1,0:T(8,128)(2,1)S(1)}, bf16[768,512]{1,0:T(8,128)(2,1)S(1)}, bf16[4,4096,128]{2,1,0:T(8,128)(2,1)S(1)}, bf16[4,256,2048]{2,...) custom-call(bf16[1,4096]{1,0:T(2,128)(2,1)S(1)} %broadcast_in_dim.9.gain, bf16[128,4096]{1,0:T(8,128)(2,1)} %hid_far.3, ...), custom_call_target="tpu_custom_call" | custom-call | tf_op jit(solution)/shard_map/gather_project/pallas_call | solution.py:568
  70.5 30.3 %attend.1 = bf16[512,1024]{1,0:T(8,128)(2,1)S(1)} custom-call(f32[16,512]{1,0:T(8,128)S(1)} %get-tuple-element.11.table, f32[8,768]{1,0:T(8,128)S(1)} %get-tuple-element.12.key_table, bf16[512,1024]{1,0:T(8,128)(2,1)S(1)} %get-tuple-element.13.q, bf16[768,512]{1,0:T(8,128)(2,1)S(1)} %get-tuple-element.14.kv, bf16[4,4096,128]{2,1,0:T(8,128)(2,1)S(1)} %get-tuple-element.15.pfx), custom_call_target="tpu_custom_call" | custom-call | tf_op jit(solution)/shard_map/attend/pallas_call | solution.py:614
  100.8 44.0 %project_reduce.1 = bf16[128,4096]{1,0:T(8,128)(2,1)S(1)} custom-call(bf16[4,128,1024]{2,1,0:T(8,128)(2,1)S(1)} %bitcast.3, bf16[4,256,2048]{2,1,0:T(8,128)(2,1)S(1)} %get-tuple-element.16.wo_low, bf16[256,4096]{1,0:T(8,128)(2,1)} %wo.3, bf16[128,4096]{1,0:T(8,128)(2,1)} %hid_far.3), custom_call_target="tpu_custom_call" | custom-call | tf_op jit(solution)/shard_map/project_reduce/pallas_call | solution.py:634
  144.8 1.0 copy.11

commit v4 on v3

--- a/solution.py
+++ b/solution.py
@@ -335,23 +335,23 @@
         for slot in range(SIDE):
             halo_copy(slot).start()
 
-    extra = {3: describe_tokens, 12: keys_and_values}
+    extra = {3: describe_tokens, 13: keys_and_values}
     for s in range(SIDE):
-        extra[13 + s] = functools.partial(project_q, s)
+        extra[14 + s] = functools.partial(project_q, s)
     lag = 2
-    ahead = 3
+    ahead = 8
     for k in range(ahead):
         x_own(k)
-    for t in range(3 * len(units) + lag):
+    for t in range(max(3 * len(units) + lag, 18)):
         if t < 3 * len(units):
             for i in Y_ROUNDS[t % 3]:
                 units[t // 3].along_y(i)
             if t % 3 == 0 and t // 3 + 1 < len(units):
                 units[t // 3 + 1].start()
-        if t < 3 * per_half:
-            x_got(t)
-            x_own(t + ahead)
-        if t >= lag:
+        if 1 <= t < 3 * per_half + 1:
+            x_got(t - 1)
+            x_own(t - 1 + ahead)
+        if lag <= t < 3 * len(units) + lag:
             for i in X_ROUNDS[(t - lag) % 3]:
                 units[(t - lag) // 3].along_x(i)
         if t in extra:
@@ -369,10 +369,17 @@
         unit.sent()
 
 
-def attend(table, key_table, q, kv, pfx, out, perm, qs, kvs, ranges, outs, top, total, acc):
+TILE = 128
+NEW_KEYS = 256
+PREFIX_KEYS = 512
+
+
+def attend(
+    table, key_table, q, kv, pfx, out,
+    perm, qs, kvs, ranges, outs, top, acc, new_scores, prefix_scores,
+):
     tokens, news, prefix = q.shape[0], kv.shape[0], pfx.shape[1]
-    tile, keys, group = 64, 256, 4
-    lanes = group * tile
+    group = 4
     exponent = math.log2(math.e) / math.sqrt(HEAD)
 
     def one_hot(flags):
@@ -380,27 +387,27 @@
 
     rank = table[8:9, :]
     spots = lax.broadcasted_iota(jnp.int32, (tokens, tokens), 0).astype(F32)
-    qs[...] = jnp.dot(one_hot(spots == rank), q[...], preferred_element_type=F32).astype(BF16)
+    by_doc = one_hot(spots == rank)
+    qs[...] = jnp.dot(by_doc, q[...], preferred_element_type=F32).astype(BF16)
+    got = lax.dot_general(
+        by_doc, table[...].astype(BF16), (((1,), (1,)), ((), ())), preferred_element_type=F32
+    )
+    for k in range(4):
+        column = 64.0 * got[:, k : k + 1] + got[:, k + 4 : k + 5]
+        ranges[k] = jnp.broadcast_to(column, (tokens, 128)).astype(jnp.int32)
     spots = lax.broadcasted_iota(jnp.int32, (news, news), 0).astype(F32)
     kvs[...] = jnp.dot(
         one_hot(spots == key_table[0:1, :]), kv[...], preferred_element_type=F32
     ).astype(BF16)
     tall = spread_rows(rank)
     lane = lax.broadcasted_iota(jnp.int32, (tokens, 128), 1)
-    rows = table[...].astype(BF16)
-    for i in range(tokens // tile):
-        flags = one_hot(tall == ((lane % tile) + tile * i).astype(F32))
-        got = jnp.dot(rows, flags, preferred_element_type=F32)
-        got = 64.0 * got[0:8] + jnp.concatenate([got[4:8]] * 2, axis=0)
-        ranges[i] = jnp.concatenate([got] * (lanes // 128), axis=1)
     for c in range(tokens // 128):
         perm[:, pl.ds(128 * c, 128)] = one_hot(tall == (lane + 128 * c).astype(F32))
 
-    @pl.loop(0, tokens // tile)
+    @pl.loop(0, tokens // TILE)
     def _(i):
-        cut = pl.ds(pl.multiple_of(i * tile, tile), tile)
+        cut = pl.ds(pl.multiple_of(i * TILE, TILE), TILE)
         top[...] = jnp.full(top.shape, MASKED, F32)
-        total[...] = jnp.zeros(total.shape, F32)
         acc[...] = jnp.zeros(acc.shape, F32)
         queries = [
             jnp.concatenate(
@@ -409,49 +416,71 @@
             for h in range(2)
         ]
 
-        def sweep(low, high, size, load):
-            first = jnp.min(low).astype(jnp.int32) // 128 * 128
-            last = jnp.max(high).astype(jnp.int32)
-
-            @pl.loop(0, (last - first + keys - 1) // keys)
+        def extent(kind, keys):
+            first = jnp.min(ranges[kind, cut, :]) // 128 * 128
+            last = jnp.max(ranges[kind + 1, cut, :])
+            return first, (last - first + keys - 1) // keys
+
+        def begin_at(first, j, keys, size):
+            return pl.multiple_of(jnp.minimum(first + j * keys, size - keys), 128)
+
+        def score(kind, where, keys, size, load, scores):
+            first, steps = where
+
+            @pl.loop(0, steps)
             def _(j):
-                begin = first + j * keys
-                start = pl.multiple_of(jnp.minimum(begin, size - keys), 128)
-                at = lax.broadcasted_iota(jnp.int32, (keys, lanes), 0)
-                near = jnp.maximum(low.astype(jnp.int32), begin) - start
-                far = high.astype(jnp.int32) - start
-                allowed = (at >= near) & (at < far)
+                start = begin_at(first, j, keys, size)
+                near = jnp.maximum(ranges[kind, cut, :], first + j * keys) - start
+                far = ranges[kind + 1, cut, :] - start
+                at = lax.broadcasted_iota(jnp.int32, (TILE, 128), 1)
+                bias = jnp.concatenate(
+                    [
+                        jnp.where((at + c >= near) & (at + c < far), 0.0, MASKED)
+                        for c in range(0, keys, 128)
+                    ],
+                    axis=1,
+                )
+                bias = jnp.concatenate([bias] * group, axis=0)
                 for h in range(2):
-                    key, value = load(h, pl.ds(start, keys))
-                    s = lax.dot_general(
-                        key, queries[h], (((1,), (1,)), ((), ())), preferred_element_type=F32
+                    s = bias + lax.dot_general(
+                        queries[h],
+                        load(2 * h, pl.ds(start, keys)),
+                        (((1,), (1,)), ((), ())),
+                        preferred_element_type=F32,
                     )
-                    s = jnp.where(allowed, s * exponent, MASKED)
-                    old = top[h, 0:1, :]
-                    new = jnp.maximum(old, jnp.max(s, axis=0, keepdims=True))
-                    p = jnp.exp2(s - new)
-                    fade = jnp.exp2(old - new)
-                    top[h, 0:1, :] = new
-                    total[h, 0:1, :] = total[h, 0:1, :] * fade + jnp.sum(p, axis=0, keepdims=True)
-                    acc[h] = acc[h] * fade + lax.dot_general(
-                        value, p.astype(BF16), (((0,), (0,)), ((), ())), preferred_element_type=F32
-                    )
-
-        got = ranges[i]
-        sweep(
-            got[2:3],
-            got[3:4],
-            news,
-            lambda h, at: (
-                kvs[at, pl.ds(2 * HEAD * h, HEAD)],
-                kvs[at, pl.ds(2 * HEAD * h + HEAD, HEAD)],
-            ),
-        )
-        sweep(got[0:1], got[1:2], prefix, lambda h, at: (pfx[2 * h, at, :], pfx[2 * h + 1, at, :]))
+                    scores[h, j] = s
+                    best = top[h]
+                    for c in range(0, keys, 128):
+                        best = jnp.maximum(best, s[:, c : c + 128])
+                    top[h] = best
+
+        def weigh(where, keys, size, load, scores):
+            first, steps = where
+
+            @pl.loop(0, steps)
+            def _(j):
+                start = begin_at(first, j, keys, size)
+                for h in range(2):
+                    best = jnp.concatenate([top[h]] * (keys // 128), axis=1)
+                    p = jnp.exp2((scores[h, j] - best) * exponent).astype(BF16)
+                    value = load(2 * h + 1, pl.ds(start, keys))
+                    value = jnp.concatenate([value, jnp.ones_like(value)], axis=1)
+                    acc[h] += jnp.dot(p, value, preferred_element_type=F32)
+
+        load_new = lambda column, at: kvs[at, pl.ds(HEAD * column, HEAD)]
+        load_prefix = lambda column, at: pfx[column, at, :]
+        own, doc = extent(2, NEW_KEYS), extent(0, PREFIX_KEYS)
+        score(2, own, NEW_KEYS, news, load_new, new_scores)
+        score(0, doc, PREFIX_KEYS, prefix, load_prefix, prefix_scores)
         for h in range(2):
-            done = jnp.transpose(acc[h] / total[h, 0:1, :]).astype(BF16)
+            best = jnp.max(top[h], axis=1, keepdims=True)
+            top[h] = jnp.broadcast_to(best, top.shape[1:])
+        weigh(own, NEW_KEYS, news, load_new, new_scores)
+        weigh(doc, PREFIX_KEYS, prefix, load_prefix, prefix_scores)
+        for h in range(2):
+            done = (acc[h, :, pl.ds(0, HEAD)] / acc[h, :, pl.ds(HEAD, HEAD)]).astype(BF16)
             for n in range(group):
-                outs[cut, pl.ds(HEAD * (group * h + n), HEAD)] = done[n * tile : (n + 1) * tile]
+                outs[cut, pl.ds(HEAD * (group * h + n), HEAD)] = done[n * TILE : (n + 1) * TILE]
 
     out[...] = jnp.dot(perm[...], outs[...], preferred_element_type=F32).astype(BF16)
 
@@ -620,13 +649,14 @@
             pltpu.VMEM((tokens, tokens), BF16),
             pltpu.VMEM((tokens, 8 * HEAD), BF16),
             pltpu.VMEM((news, 4 * HEAD), BF16),
-            pltpu.VMEM((8, 8, 256), F32),
+            pltpu.VMEM((4, tokens, 128), jnp.int32),
             pltpu.VMEM((tokens, 8 * HEAD), BF16),
-            pltpu.VMEM((2, 8, 256), F32),
-            pltpu.VMEM((2, 8, 256), F32),
-            pltpu.VMEM((2, HEAD, 256), F32),
+            pltpu.VMEM((2, 4 * TILE, 128), F32),
+            pltpu.VMEM((2, 4 * TILE, 2 * HEAD), F32),
+            pltpu.VMEM((2, news // NEW_KEYS, 4 * TILE, NEW_KEYS), F32),
+            pltpu.VMEM((2, prefix_len // PREFIX_KEYS, 4 * TILE, PREFIX_KEYS), F32),
         ],
-        compiler_params=pltpu.CompilerParams(vmem_limit_bytes=32 * 2**20),
+        compiler_params=pltpu.CompilerParams(vmem_limit_bytes=40 * 2**20),
         name="attend",
     )(table, key_table, q, kv, pfx)
 

time: 147 us -> 124 us (0.84)
  Pallas kernels: 144 us -> 121 us
    pallas_call x1, Pallas kernels: 30.3 us -> 18.4 us  [local(): pl.pallas_call(attend, out_shape=jax.ShapeDtypeStruct((tokens, 8 * HEAD),...]
    pallas_call x1, Pallas kernels: 44 us -> 37.9 us  [local(): pl.pallas_call(project_reduce, out_shape=jax.ShapeDtypeStruct(hidden_in.s...]
    pallas_call x1, Pallas kernels: 69.8 us -> 64.2 us  [local(): pl.pallas_call(gather_project, out_shape=(jax.ShapeDtypeStruct((tokens, 8...]
where the time goes in v4:
time: 124 us; the launch traced here: 122 us
  Pallas kernels  121 us (98%)
  local copies, waits for them, and re-layouts  1.68 us (1%)
    pallas_call x1, Pallas kernels, local(): pl.pallas_call(gather_project, out_shape=(jax.ShapeDtypeStruct((tokens, 8...  64.2 us
    pallas_call x1, Pallas kernels, local(): pl.pallas_call(project_reduce, out_shape=jax.ShapeDtypeStruct(hidden_in.s...  37.9 us
    pallas_call x1, Pallas kernels, local(): pl.pallas_call(attend, out_shape=jax.ShapeDtypeStruct((tokens, 8 * HEAD),...  18.4 us

profile of v4, /device:TPU:0, one launch (start us, length us, event | category | flops | bytes accessed | tf_op | source)
XLA Modules:
  0.0 122.3 jit_solution(9901802313202410613)
XLA Ops:
  0.0 0.7 broadcast_in_dim.9.gain
  0.7 64.2 %gather_project.1 = (bf16[512,1024]{1,0:T(8,128)(2,1)S(1)}, bf16[768,512]{1,0:T(8,128)(2,1)S(1)}, bf16[4,4096,128]{2,1,0:T(8,128)(2,1)S(1)}, bf16[4,256,2048]{2,...) custom-call(bf16[1,4096]{1,0:T(2,128)(2,1)S(1)} %broadcast_in_dim.9.gain, bf16[128,4096]{1,0:T(8,128)(2,1)} %hid_far.3, ...), custom_call_target="tpu_custom_call" | custom-call | tf_op jit(solution)/shard_map/gather_project/pallas_call | solution.py:597
  64.9 18.4 %attend.1 = bf16[512,1024]{1,0:T(8,128)(2,1)S(1)} custom-call(f32[16,512]{1,0:T(8,128)S(1)} %get-tuple-element.11.table, f32[8,768]{1,0:T(8,128)S(1)} %get-tuple-element.12.key_table, bf16[512,1024]{1,0:T(8,128)(2,1)S(1)} %get-tuple-element.13.q, bf16[768,512]{1,0:T(8,128)(2,1)S(1)} %get-tuple-element.14.kv, bf16[4,4096,128]{2,1,0:T(8,128)(2,1)S(1)} %get-tuple-element.15.pfx), custom_call_target="tpu_custom_call" | custom-call | tf_op jit(solution)/shard_map/attend/pallas_call | solution.py:643
  83.3 37.9 %project_reduce.1 = bf16[128,4096]{1,0:T(8,128)(2,1)S(1)} custom-call(bf16[4,128,1024]{2,1,0:T(8,128)(2,1)S(1)} %bitcast.3, bf16[4,256,2048]{2,1,0:T(8,128)(2,1)S(1)} %get-tuple-element.16.wo_low, bf16[256,4096]{1,0:T(8,128)(2,1)} %wo.3, bf16[128,4096]{1,0:T(8,128)(2,1)} %hid_far.3), custom_call_target="tpu_custom_call" | custom-call | tf_op jit(solution)/shard_map/project_reduce/pallas_call | solution.py:664
  121.3 1.0 copy.11

commit v5 on v4

--- a/solution.py
+++ b/solution.py
@@ -278,28 +278,29 @@
                 x_copy(side, n, d).start()
 
     tokens = SIDE * 128
-    half_rows = 2 * 128
-
-    def project_kv():
-        for s in range(SIDE):
-            @pl.loop(0, 2)
-            def _(m):
-                tall = pl.ds(pl.multiple_of(m * half_rows, half_rows), half_rows)
-                lhs = xs[pl.ds(2 * m, 2)].reshape(half_rows, xs.shape[2])
-                got = jnp.dot(lhs, wkvs[s], preferred_element_type=F32)
-                if s % 2 == 0:
-                    got = rotate(got, cos[tall, :], sin[tall, :])
-                kv[tall, pl.ds(HEAD * s, HEAD)] = got.astype(BF16)
-
-    def project_q(s):
-        @pl.loop(0, 2)
-        def _(m):
-            tall = pl.ds(pl.multiple_of(m * half_rows, half_rows), half_rows)
-            lhs = xs[pl.ds(2 * m, 2)].reshape(half_rows, xs.shape[2])
-            got = jnp.dot(lhs, wqs[s], preferred_element_type=F32)
-            for n in range(2):
-                one = rotate(got[:, HEAD * n : HEAD * (n + 1)], cos[tall, :], sin[tall, :])
-                q_out[tall, pl.ds(HEAD * (2 * s + n), HEAD)] = one.astype(BF16)
+    def both(ds):
+        return jnp.concatenate([xs[(z + d) % SIDE] for d in ds], axis=0)
+
+    def group(d):
+        return pl.ds(pl.multiple_of((z + d) % SIDE * 128, 128), 128)
+
+    def project_kv(ds):
+        for h in range(2):
+            weight = jnp.concatenate([wkvs[2 * h], wkvs[2 * h + 1]], axis=1)
+            got = jnp.dot(both(ds), weight, preferred_element_type=F32)
+            for n, d in enumerate(ds):
+                part, at = got[128 * n : 128 * (n + 1)], group(d)
+                key = rotate(part[:, :HEAD], cos[at, :], sin[at, :])
+                kv[at, pl.ds(2 * HEAD * h, HEAD)] = key.astype(BF16)
+                kv[at, pl.ds(2 * HEAD * h + HEAD, HEAD)] = part[:, HEAD:].astype(BF16)
+
+    def project_q(ds, s):
+        got = jnp.dot(both(ds), wqs[s], preferred_element_type=F32)
+        for n, d in enumerate(ds):
+            part, at = got[128 * n : 128 * (n + 1)], group(d)
+            for m in range(2):
+                one = rotate(part[:, HEAD * m : HEAD * (m + 1)], cos[at, :], sin[at, :])
+                q_out[at, pl.ds(HEAD * (2 * s + m), HEAD)] = one.astype(BF16)
 
     def halo_copy(slot):
         dst = (slot + y // 3) % SIDE
@@ -326,18 +327,34 @@
         turn = jnp.sin(angle)
         sin[...] = jnp.where(lane < HEAD // 2, -turn, turn)
 
-    def keys_and_values():
-        for k in range(4, 6):
-            stays[k].wait()
-        for unit in units[:3]:
+    early, late = (0, 1), (3, 2)
+
+    def early_kv():
+        stays[4].wait()
+        units[0].sibling()
+        project_kv(early)
+
+    def early_q():
+        stays[5].wait()
+        for unit in units[1:3]:
             unit.sibling()
-        project_kv()
+        project_q(early, 0)
+        project_q(early, 1)
+
+    def late_kv():
+        project_kv(late)
         for slot in range(SIDE):
             halo_copy(slot).start()
 
-    extra = {3: describe_tokens, 13: keys_and_values}
-    for s in range(SIDE):
-        extra[14 + s] = functools.partial(project_q, s)
+    extra = {
+        3: [describe_tokens],
+        9: [early_kv],
+        11: [early_q],
+        12: [lambda: project_q(early, 2), lambda: project_q(early, 3)],
+        13: [late_kv],
+        14: [lambda: project_q(late, 0), lambda: project_q(late, 1)],
+        15: [lambda: project_q(late, 2), lambda: project_q(late, 3)],
+    }
     lag = 2
     ahead = 8
     for k in range(ahead):
@@ -354,8 +371,8 @@
         if lag <= t < 3 * len(units) + lag:
             for i in X_ROUNDS[(t - lag) % 3]:
                 units[(t - lag) // 3].along_x(i)
-        if t in extra:
-            extra[t]()
+        for work in extra.get(t, []):
+            work()
     for unit in units[3:]:
         unit.sibling()
     for k in range(6, 8):

time: 124 us -> 120 us (0.968)
  Pallas kernels: 121 us -> 116 us
    pallas_call x1, Pallas kernels: 64.2 us -> 59.1 us  [local(): pl.pallas_call(gather_project, out_shape=(jax.ShapeDtypeStruct((tokens, 8...]
where the time goes in v5:
time: 120 us; the launch traced here: 118 us
  Pallas kernels  116 us (97%)
  local copies, waits for them, and re-layouts  1.68 us (1%)
    pallas_call x1, Pallas kernels, local(): pl.pallas_call(gather_project, out_shape=(jax.ShapeDtypeStruct((tokens, 8...  59.1 us
    pallas_call x1, Pallas kernels, local(): pl.pallas_call(project_reduce, out_shape=jax.ShapeDtypeStruct(hidden_in.s...  38.8 us
    pallas_call x1, Pallas kernels, local(): pl.pallas_call(attend, out_shape=jax.ShapeDtypeStruct((tokens, 8 * HEAD),...  18.4 us

profile of v5, /device:TPU:0, one launch (start us, length us, event | category | flops | bytes accessed | tf_op | source)
XLA Modules:
  0.0 118.0 jit_solution(13867641054302759217)
XLA Ops:
  0.0 0.7 broadcast_in_dim.9.gain
  0.7 59.1 %gather_project.1 = (bf16[512,1024]{1,0:T(8,128)(2,1)S(1)}, bf16[768,512]{1,0:T(8,128)(2,1)S(1)}, bf16[4,4096,128]{2,1,0:T(8,128)(2,1)S(1)}, bf16[4,256,2048]{2,...) custom-call(bf16[1,4096]{1,0:T(2,128)(2,1)S(1)} %broadcast_in_dim.9.gain, bf16[128,4096]{1,0:T(8,128)(2,1)} %hid_far.3, ...), custom_call_target="tpu_custom_call" | custom-call | tf_op jit(solution)/shard_map/gather_project/pallas_call | solution.py:614
  59.8 18.4 %attend.1 = bf16[512,1024]{1,0:T(8,128)(2,1)S(1)} custom-call(f32[16,512]{1,0:T(8,128)S(1)} %get-tuple-element.11.table, f32[8,768]{1,0:T(8,128)S(1)} %get-tuple-element.12.key_table, bf16[512,1024]{1,0:T(8,128)(2,1)S(1)} %get-tuple-element.13.q, bf16[768,512]{1,0:T(8,128)(2,1)S(1)} %get-tuple-element.14.kv, bf16[4,4096,128]{2,1,0:T(8,128)(2,1)S(1)} %get-tuple-element.15.pfx), custom_call_target="tpu_custom_call" | custom-call | tf_op jit(solution)/shard_map/attend/pallas_call | solution.py:660
  78.2 38.8 %project_reduce.1 = bf16[128,4096]{1,0:T(8,128)(2,1)S(1)} custom-call(bf16[4,128,1024]{2,1,0:T(8,128)(2,1)S(1)} %bitcast.3, bf16[4,256,2048]{2,1,0:T(8,128)(2,1)S(1)} %get-tuple-element.16.wo_low, bf16[256,4096]{1,0:T(8,128)(2,1)} %wo.3, bf16[128,4096]{1,0:T(8,128)(2,1)} %hid_far.3), custom_call_target="tpu_custom_call" | custom-call | tf_op jit(solution)/shard_map/project_reduce/pallas_call | solution.py:681
  117.0 1.0 copy.11

commit v6 on v5

--- a/solution.py
+++ b/solution.py
@@ -196,9 +196,9 @@
 
 
 def gather_project(
-    gain, hid_far, seg_ids_far, seg_doc_far, doc_lens_far, wq, wkv, pfx, wo,
+    gain_far, hid_far, seg_ids_far, seg_doc_far, doc_lens_far, wq, wkv, pfx, wo,
     q_out, kv, pfx_all, wo_low, table, key_table,
-    xs, wqs, wkvs, cos, sin, hid, seg_ids, seg_doc, doc_lens,
+    xs, wqs, wkvs, cos, sin, gain, hid, seg_ids, seg_doc, doc_lens,
     send, recv, x_send, x_recv, halo_send, halo_recv, stay,
 ):
     x, core, z, y = place()
@@ -211,6 +211,7 @@
         for k, (src, dst) in enumerate(
             [
                 (hid_far, hid),
+                (gain_far, gain),
                 (seg_ids_far, seg_ids),
                 (seg_doc_far, seg_doc),
                 (doc_lens_far, doc_lens),
@@ -242,9 +243,12 @@
     units[0].start()
 
     stays[0].wait()
+    stays[1].wait()
     values = hid[...].astype(F32)
     scale = lax.rsqrt(jnp.mean(values * values, axis=-1, keepdims=True) + EPS)
-    xs[z] = (values * scale * gain[...].astype(F32)).astype(BF16)
+    wide = gain[...].astype(F32)
+    wide = jnp.concatenate([wide[r : r + 1, :] for r in range(wide.shape[0])], axis=1)
+    xs[z] = (values * scale * wide).astype(BF16)
 
     per_half = HALO // PIECE
 
@@ -313,16 +317,19 @@
         )
 
     def describe_tokens():
-        for k in range(1, 4):
+        for k in range(2, 5):
             stays[k].wait()
         rows, key_rows, pos = describe(seg_ids, seg_doc, doc_lens, y)
         table[...] = rows
         key_table[...] = key_rows
+        cos[...] = spread_rows(pos)
+
+    def rotary_tables():
         lane = lax.broadcasted_iota(jnp.int32, (1, HEAD), 1)
         inverse = jnp.zeros((1, HEAD), F32)
         for i in range(HEAD // 2):
             inverse = jnp.where(lane % (HEAD // 2) == i, THETA ** (-2.0 * i / HEAD), inverse)
-        angle = (pfx.shape[0] + spread_rows(pos)) * inverse
+        angle = (pfx.shape[0] + cos[...]) * inverse
         cos[...] = jnp.cos(angle)
         turn = jnp.sin(angle)
         sin[...] = jnp.where(lane < HEAD // 2, -turn, turn)
@@ -330,12 +337,12 @@
     early, late = (0, 1), (3, 2)
 
     def early_kv():
-        stays[4].wait()
+        stays[5].wait()
         units[0].sibling()
         project_kv(early)
 
     def early_q():
-        stays[5].wait()
+        stays[6].wait()
         for unit in units[1:3]:
             unit.sibling()
         project_q(early, 0)
@@ -348,6 +355,7 @@
 
     extra = {
         3: [describe_tokens],
+        6: [rotary_tables],
         9: [early_kv],
         11: [early_q],
         12: [lambda: project_q(early, 2), lambda: project_q(early, 3)],
@@ -375,7 +383,7 @@
             work()
     for unit in units[3:]:
         unit.sibling()
-    for k in range(6, 8):
+    for k in range(7, 9):
         stays[k].wait()
     for slot in range(SIDE):
         halo_copy(slot).wait()
@@ -387,7 +395,7 @@
 
 
 TILE = 128
-NEW_KEYS = 256
+NEW_KEYS = 384
 PREFIX_KEYS = 512
 
 
@@ -536,13 +544,13 @@
         return jnp.dot(att[slot % SIDE], weight, preferred_element_type=F32)
 
     def far(j):
-        return remote(far_out.at[j], far_in.at[j], far_send.at[j], far_recv.at[j], sides[j % 2])
+        return remote(far_out.at[j], far_in.at[j], far_send.at[0], far_recv.at[j], sides[j % 2])
 
     def near(side, j):
         return remote(
             near_out.at[side, j],
             near_in.at[side, j],
-            near_send.at[side, j],
+            near_send.at[0],
             near_recv.at[side, j],
             sides[side],
         )
@@ -571,15 +579,18 @@
 
     for j in range(chunks // 2):
         far_step(j)
+    step = chunks // 8
     along_y(0)
-    near_step(0)
-    near_step(1)
+    for j in range(2 * step):
+        near_step(j)
     along_y(1)
     along_x(0)
-    near_step(2)
+    for j in range(2 * step, 3 * step):
+        near_step(j)
     along_y(2)
     along_x(1)
-    near_step(3)
+    for j in range(3 * step, 4 * step):
+        near_step(j)
     along_x(2)
     stays[0].wait()
     unit.sibling()
@@ -595,10 +606,8 @@
         near(1, j).wait_recv()
         mine = mine + near_in[0, j].astype(F32) + near_in[1, j].astype(F32)
         mixed[:, cut] = mine.astype(BF16)
-    for j in range(chunks):
-        far(j).wait_send()
-        near(0, j).wait_send()
-        near(1, j).wait_send()
+    remote(far_out, far_in, far_send.at[0], far_recv.at[0], sides[0]).wait_send()
+    remote(near_out, near_in, near_send.at[0], near_recv.at[0, 0], sides[0]).wait_send()
     unit.sent()
 
 
@@ -621,7 +630,7 @@
             jax.ShapeDtypeStruct((16, tokens), F32),
             jax.ShapeDtypeStruct((8, news), F32),
         ),
-        in_specs=[vmem] + [whole] * 8,
+        in_specs=[whole] * 9,
         out_specs=(vmem,) * 6,
         scratch_shapes=[
             pltpu.VMEM((SIDE, 128, width), BF16),
@@ -629,6 +638,7 @@
             pltpu.VMEM((SIDE,) + keyvalue_weight.shape, BF16),
             pltpu.VMEM((tokens, HEAD), F32),
             pltpu.VMEM((tokens, HEAD), F32),
+            pltpu.VMEM((width // 128, 128), BF16),
             pltpu.VMEM(hidden_in.shape, BF16),
             pltpu.VMEM((1,) + seg_ids.shape, jnp.int32),
             pltpu.VMEM((1,) + seg_doc.shape, jnp.int32),
@@ -639,14 +649,14 @@
             pltpu.SemaphoreType.DMA((2, 16)),
             pltpu.SemaphoreType.DMA((4,)),
             pltpu.SemaphoreType.DMA((4,)),
-            pltpu.SemaphoreType.DMA((8,)),
+            pltpu.SemaphoreType.DMA((9,)),
         ],
         compiler_params=pltpu.CompilerParams(
             collective_id=0, has_side_effects=True, vmem_limit_bytes=30 * 2**20
         ),
         name="gather_project",
     )(
-        norm_gain[None, :],
+        far(norm_gain.reshape(-1, 128)),
         far(hidden_in),
         far(seg_ids[None, :]),
         far(seg_doc[None, :]),
@@ -670,7 +680,7 @@
             pltpu.VMEM((tokens, 8 * HEAD), BF16),
             pltpu.VMEM((2, 4 * TILE, 128), F32),
             pltpu.VMEM((2, 4 * TILE, 2 * HEAD), F32),
-            pltpu.VMEM((2, news // NEW_KEYS, 4 * TILE, NEW_KEYS), F32),
+            pltpu.VMEM((2, pl.cdiv(news, NEW_KEYS), 4 * TILE, NEW_KEYS), F32),
             pltpu.VMEM((2, prefix_len // PREFIX_KEYS, 4 * TILE, PREFIX_KEYS), F32),
         ],
         compiler_params=pltpu.CompilerParams(vmem_limit_bytes=40 * 2**20),
@@ -690,9 +700,9 @@
             pltpu.VMEM((2, chunks, 128, COLS), BF16),
             pltpu.VMEM((chunks, 128, COLS), BF16),
             pltpu.VMEM((2, chunks, 128, COLS), BF16),
+            pltpu.SemaphoreType.DMA((1,)),
             pltpu.SemaphoreType.DMA((chunks,)),
-            pltpu.SemaphoreType.DMA((chunks,)),
-            pltpu.SemaphoreType.DMA((2, chunks)),
+            pltpu.SemaphoreType.DMA((1,)),
             pltpu.SemaphoreType.DMA((2, chunks)),
             pltpu.SemaphoreType.DMA((1,)),
             pltpu.SemaphoreType.DMA((1, 13)),

time: 120 us -> 119 us (level)
    pallas_call x1, Pallas kernels: 38.8 us -> 40.2 us  [local(): pl.pallas_call(project_reduce, out_shape=jax.ShapeDtypeStruct(hidden_in.s...]
where the time goes in v6:
time: 119 us; the launch traced here: 118 us
  Pallas kernels  117 us (98%)
    pallas_call x1, Pallas kernels, local(): pl.pallas_call(gather_project, out_shape=(jax.ShapeDtypeStruct((tokens, 8...  58.9 us
    pallas_call x1, Pallas kernels, local(): pl.pallas_call(project_reduce, out_shape=jax.ShapeDtypeStruct(hidden_in.s...  40.2 us
    pallas_call x1, Pallas kernels, local(): pl.pallas_call(attend, out_shape=jax.ShapeDtypeStruct((tokens, 8 * HEAD),...  17.8 us

profile of v6, /device:TPU:0, one launch (start us, length us, event | category | flops | bytes accessed | tf_op | source)
XLA Modules:
  0.0 117.8 jit_solution(13945745291533132103)
XLA Ops:
  0.0 58.9 %gather_project.1 = (bf16[512,1024]{1,0:T(8,128)(2,1)S(1)}, bf16[768,512]{1,0:T(8,128)(2,1)S(1)}, bf16[4,4096,128]{2,1,0:T(8,128)(2,1)S(1)}, bf16[4,256,2048]{2,...) custom-call(bf16[32,128]{1,0:T(8,128)(2,1)} %bitcast.5, bf16[128,4096]{1,0:T(8,128)(2,1)} %hid_far.3, ...), custom_call_target="tpu_custom_call" | custom-call | tf_op jit(solution)/shard_map/gather_project/pallas_call | solution.py:623
  58.9 17.8 %attend.1 = bf16[512,1024]{1,0:T(8,128)(2,1)S(1)} custom-call(f32[16,512]{1,0:T(8,128)S(1)} %get-tuple-element.11.table, f32[8,768]{1,0:T(8,128)S(1)} %get-tuple-element.12.key_table, bf16[512,1024]{1,0:T(8,128)(2,1)S(1)} %get-tuple-element.13.q, bf16[768,512]{1,0:T(8,128)(2,1)S(1)} %get-tuple-element.14.kv, bf16[4,4096,128]{2,1,0:T(8,128)(2,1)S(1)} %get-tuple-element.15.pfx), custom_call_target="tpu_custom_call" | custom-call | tf_op jit(solution)/shard_map/attend/pallas_call | solution.py:670
  76.7 40.2 %project_reduce.1 = bf16[128,4096]{1,0:T(8,128)(2,1)S(1)} custom-call(bf16[4,128,1024]{2,1,0:T(8,128)(2,1)S(1)} %bitcast.4, bf16[4,256,2048]{2,1,0:T(8,128)(2,1)S(1)} %get-tuple-element.16.wo_low, bf16[256,4096]{1,0:T(8,128)(2,1)} %wo.3, bf16[128,4096]{1,0:T(8,128)(2,1)} %hid_far.3), custom_call_target="tpu_custom_call" | custom-call | tf_op jit(solution)/shard_map/project_reduce/pallas_call | solution.py:691
  116.9 1.0 copy.11
